TPU v7x, 256 devices: a whole 4x4x8 slice. The times are simulated.
256 devices in a mesh: seq: 32 (over y, z), head: 8 (over x, core).
Axes of the slice: x: 4, y: 4, z: 8, core: 2. Of those that a mesh axis runs over, the one named last changes fastest.
Arguments:
- frames: bfloat16 [98304, 8192], P('seq', 'head'), may hold values from -6 to 6
- state_proj: bfloat16 [256, 98304], P('head', 'seq'), as said below
- log_decay: float32 [128, 98304], P('head', 'seq'), may hold values from -0.7 to 0
- skip_gain: float32 [128], P('head'), may hold values from 0.1 to 1.9
- group_pos: int32 [384], P('seq'), may hold values from 0 to 383, as said below
Outputs:
- mixed: bfloat16 [98304, 8192], P('seq', 'head')
Inputs may be any that keep to these rules, and one draw needn't show every extreme that they name: `group_pos`: device d of seq holds in its 12 slots the groups of sequence positions d * 12 to (d + 1) * 12 - 1, each once, in an order drawn from the seed. `state_proj`: entries lie within 5 times their scale, which is the inverse fourth root of 393216.
All inputs are finite; a program needn't handle non-finite values.
Results may differ from a plain program's by a relative error of at most 0.0053.
Values may be sent and summed in bfloat16 or wider, within the bound.
No kernel may reach another device: no remote copies, remote signals or barrier semaphores. Data moves between devices by JAX's collectives and lax.ppermute only.
A program may use at most 128 MiB of HBM per device.

v0:
```python
import jax
import jax.numpy as jnp
from jax import lax
from jax.sharding import PartitionSpec as P

HEAD_DIM = 64
STATE = 128
GROUP = 256


def passed_along(value, axis, steps):
    count = lax.axis_size(axis)
    initial, last = (max(0, -steps), min(count, count - steps))
    return lax.ppermute(value, axis, [(source, source + steps) for source in range(initial, last)])


def prefix_matrix(length):
    step_ids = jnp.arange(length)
    return (step_ids[:, None] <= step_ids[None, :]).astype(jnp.float32)


def group_terms(inputs, group_in, natlog_speeds, upper):
    running = jnp.dot(natlog_speeds, upper, precision=lax.Precision.HIGHEST)
    input_map = group_in[:STATE]
    output_map = group_in[STATE:]
    coupling = lax.dot_general(
        output_map, input_map, (((0,), (0,)), ((), ())), preferred_element_type=jnp.float32
    )
    step_ids = jnp.arange(running.shape[1])
    causal = (step_ids[:, None] >= step_ids[None, :])[None]
    log_gap = running[:, :, None] - running[:, None, :]
    decay_table = jnp.where(causal, jnp.exp(jnp.where(causal, log_gap, 0.0)), 0.0)
    weights = (coupling[None] * decay_table).astype(jnp.bfloat16)
    within = jnp.einsum("hts,shp->thp", weights, inputs, preferred_element_type=jnp.float32)
    group_log = running[:, -1]
    carried = (inputs * jnp.exp(group_log[:, None] - running).T[:, :, None]).astype(jnp.bfloat16)
    summary = jnp.einsum("shp,ns->hpn", carried, input_map, preferred_element_type=jnp.float32)
    return (within, summary, running)


def shards(frames, state_proj, log_decay, skip_gain, group_pos):
    whole_proj = lax.all_gather(state_proj, "head", axis=0, tiled=True)
    group_count = group_pos.shape[0]
    heads_here = skip_gain.shape[0]
    ordinal_place = group_pos - lax.axis_index("seq") * group_count
    slot_ids = jnp.arange(group_count, dtype=jnp.int32)
    inverse = jnp.sum(
        jnp.where(ordinal_place[:, None] == slot_ids[None, :], slot_ids[:, None], 0), axis=0
    )
    inputs = frames.reshape(group_count, GROUP, heads_here, HEAD_DIM)[inverse]
    projections = whole_proj.reshape(2 * STATE, group_count, GROUP).transpose(1, 0, 2)[inverse]
    natlog_speeds = log_decay.reshape(heads_here, group_count, GROUP).transpose(1, 0, 2)[inverse]
    upper = prefix_matrix(GROUP)
    within, summary, running = lax.map(
        lambda group_item: group_terms(group_item[0], group_item[1], group_item[2], upper),
        (inputs, projections, natlog_speeds),
    )
    group_log = running[:, :, -1]

    def advance(carry_state, group_item):
        return (jnp.exp(group_item[1])[:, None, None] * carry_state + group_item[0], carry_state)

    empty_state = jnp.zeros((heads_here, HEAD_DIM, STATE), jnp.float32)
    local_end, segment_prior = lax.scan(advance, empty_state, (summary, group_log))
    total_log = jnp.sum(group_log, axis=0)
    before_log = jnp.cumsum(group_log, axis=0) - group_log

    def pass_on(index_step, incoming):
        return passed_along(jnp.exp(total_log)[:, None, None] * incoming + local_end, "seq", 1)

    carry_in = lax.fori_loop(0, lax.axis_size("seq") - 1, pass_on, jnp.zeros_like(local_end))
    held_state = (jnp.exp(before_log)[:, :, None, None] * carry_in[None] + segment_prior).astype(
        jnp.bfloat16
    )
    across_shards = jnp.einsum(
        "chpn,cnt->cthp", held_state, projections[:, STATE:], preferred_element_type=jnp.float32
    )
    across_shards = across_shards * jnp.exp(running).transpose(0, 2, 1)[:, :, :, None]
    output = (
        within + across_shards + skip_gain[None, None, :, None] * inputs.astype(jnp.float32)
    ).astype(jnp.bfloat16)
    return output.reshape(group_count * GROUP, heads_here * HEAD_DIM)


def solution(mesh):
    return jax.shard_map(
        shards,
        mesh=mesh,
        in_specs=(P("seq", "head"), P("head", "seq"), P("head", "seq"), P("head"), P("seq")),
        out_specs=P("seq", "head"),
        check_vma=False,
    )
```

profile of v0, /device:TPU:30, one launch (start us, length us, event | category | flops | bytes accessed | tf_op | source)
XLA Modules:
  0.0 707.8 jit_solution(2451832417057721928)
XLA Ops:
  7.3 16.8 %reshape.107 = bf16[12,256,16,64]{3,2,1,0:T(8,128)(2,1)} reshape(bf16[3072,1024]{1,0:T(8,128)(2,1)} %param.11) | data formatting | bytes 12582912 | tf_op jit(solution)/shard_map/reshape | solution.py:50
  24.1 15.0 %copy.24 = bf16[12,256,16,64]{1,3,2,0:T(8,128)(2,1)} copy(bf16[12,256,16,64]{3,2,1,0:T(8,128)(2,1)} %reshape.107) | data formatting | bytes 12582912 | tf_op jit(solution)/shard_map/reshape | solution.py:50
  55.6 76.3 %while.41 = (s32[]{:T(128)}, f32[12,256,16,64]{1,3,2,0:T(8,128)}, f32[12,16,64,128]{3,2,1,0:T(8,128)}, f32[12,16,256]{2,1,0:T(8,128)S(1)}, bf16[12,256,16,64]{1,...) while((s32[]{:T(128)}, f32[12,256,16,64]{1,3,2,0:T(8,128)}, ...), condition=%wide.region_2.3_spmd.clone, body=%wide.region_1.2_spmd.clone.sunk | while | flops 236916736 | bytes 3609397 | solution.py:54
  138.6 24.6 %while.42 = (s32[]{:T(128)}, f32[16,64,128]{2,1,0:T(8,128)S(1)}, f32[12,16,64,128]{3,2,1,0:T(8,128)}, f32[12,16]{1,0:T(8,128)S(1)}, f32[12,16,64,128]{3,2,1,0:T(8,128)}, /*index=5*/s32[]{:T(128)}, s32[]{:T(128)}) while((s32[]{:T(128)}, f32[16,64,128]{2,1,0:T(8,128)S(1)}, f32[12,16,64,128]{3,2,1,0:T(8,128)}, ...), condition=%wide.region_5.6_spmd.clone, body=%wide.region_4.5_spmd.clone.sunk | while | flops 524291 | bytes 2622240 | solution.py:64
  164.0 492.4 %while.40 = (s32[]{:T(128)}, f32[16,64,128]{2,1,0:T(8,128)S(1)}, f32[16,1,1]{0,2,1:T(1,128)S(1)}, f32[16,64,128]{2,1,0:T(8,128)S(1)}, s32[]{:T(128)}) while((s32[]{:T(128)}, f32[16,64,128]{2,1,0:T(8,128)S(1)}, f32[16,1,1]{0,2,1:T(1,128)S(1)}, f32[16,64,128]{2,1,0:T(8,128)S(1)}, s32[]{:T(128)}) %tuple.68), condition=%wide.region_8.9_spmd, body=%wide.region_7.8_spmd.sunk | while | flops 262146 | bytes 3670181 | solution.py:71
  167.9 16.1 %collective-permute-done = f32[16,64,128]{2,1,0:T(8,128)S(1)} collective-permute-done((f32[16,64,128]{2,1,0:T(8,128)S(1)}, f32[16,64,128]{2,1,0:T(8,128)S(1)}, u32[]{:S(2)}, u32[]{:S(2)}) %collective-permute-start) | collective-permute-done | bytes 524320 | tf_op jit(solution)/shard_map/while/body/eval_jaxpr/ppermute | solution.py:14
  186.1 15.3 %collective-permute-done = f32[16,64,128]{2,1,0:T(8,128)S(1)} collective-permute-done((f32[16,64,128]{2,1,0:T(8,128)S(1)}, f32[16,64,128]{2,1,0:T(8,128)S(1)}, u32[]{:S(2)}, u32[]{:S(2)}) %collective-permute-start) | collective-permute-done | bytes 524320 | tf_op jit(solution)/shard_map/while/body/eval_jaxpr/ppermute | solution.py:14
  203.4 14.4 %collective-permute-done = f32[16,64,128]{2,1,0:T(8,128)S(1)} collective-permute-done((f32[16,64,128]{2,1,0:T(8,128)S(1)}, f32[16,64,128]{2,1,0:T(8,128)S(1)}, u32[]{:S(2)}, u32[]{:S(2)}) %collective-permute-start) | collective-permute-done | bytes 524320 | tf_op jit(solution)/shard_map/while/body/eval_jaxpr/ppermute | solution.py:14
  219.9 13.6 %collective-permute-done = f32[16,64,128]{2,1,0:T(8,128)S(1)} collective-permute-done((f32[16,64,128]{2,1,0:T(8,128)S(1)}, f32[16,64,128]{2,1,0:T(8,128)S(1)}, u32[]{:S(2)}, u32[]{:S(2)}) %collective-permute-start) | collective-permute-done | bytes 524320 | tf_op jit(solution)/shard_map/while/body/eval_jaxpr/ppermute | solution.py:14
  235.5 12.7 %collective-permute-done = f32[16,64,128]{2,1,0:T(8,128)S(1)} collective-permute-done((f32[16,64,128]{2,1,0:T(8,128)S(1)}, f32[16,64,128]{2,1,0:T(8,128)S(1)}, u32[]{:S(2)}, u32[]{:S(2)}) %collective-permute-start) | collective-permute-done | bytes 524320 | tf_op jit(solution)/shard_map/while/body/eval_jaxpr/ppermute | solution.py:14
  250.3 11.9 %collective-permute-done = f32[16,64,128]{2,1,0:T(8,128)S(1)} collective-permute-done((f32[16,64,128]{2,1,0:T(8,128)S(1)}, f32[16,64,128]{2,1,0:T(8,128)S(1)}, u32[]{:S(2)}, u32[]{:S(2)}) %collective-permute-start) | collective-permute-done | bytes 524320 | tf_op jit(solution)/shard_map/while/body/eval_jaxpr/ppermute | solution.py:14
  291.3 12.9 %collective-permute-done = f32[16,64,128]{2,1,0:T(8,128)S(1)} collective-permute-done((f32[16,64,128]{2,1,0:T(8,128)S(1)}, f32[16,64,128]{2,1,0:T(8,128)S(1)}, u32[]{:S(2)}, u32[]{:S(2)}) %collective-permute-start) | collective-permute-done | bytes 524320 | tf_op jit(solution)/shard_map/while/body/eval_jaxpr/ppermute | solution.py:14
  306.2 14.0 %collective-permute-done = f32[16,64,128]{2,1,0:T(8,128)S(1)} collective-permute-done((f32[16,64,128]{2,1,0:T(8,128)S(1)}, f32[16,64,128]{2,1,0:T(8,128)S(1)}, u32[]{:S(2)}, u32[]{:S(2)}) %collective-permute-start) | collective-permute-done | bytes 524320 | tf_op jit(solution)/shard_map/while/body/eval_jaxpr/ppermute | solution.py:14
  322.3 15.2 %collective-permute-done = f32[16,64,128]{2,1,0:T(8,128)S(1)} collective-permute-done((f32[16,64,128]{2,1,0:T(8,128)S(1)}, f32[16,64,128]{2,1,0:T(8,128)S(1)}, u32[]{:S(2)}, u32[]{:S(2)}) %collective-permute-start) | collective-permute-done | bytes 524320 | tf_op jit(solution)/shard_map/while/body/eval_jaxpr/ppermute | solution.py:14
  339.5 16.3 %collective-permute-done = f32[16,64,128]{2,1,0:T(8,128)S(1)} collective-permute-done((f32[16,64,128]{2,1,0:T(8,128)S(1)}, f32[16,64,128]{2,1,0:T(8,128)S(1)}, u32[]{:S(2)}, u32[]{:S(2)}) %collective-permute-start) | collective-permute-done | bytes 524320 | tf_op jit(solution)/shard_map/while/body/eval_jaxpr/ppermute | solution.py:14
  357.9 16.3 %collective-permute-done = f32[16,64,128]{2,1,0:T(8,128)S(1)} collective-permute-done((f32[16,64,128]{2,1,0:T(8,128)S(1)}, f32[16,64,128]{2,1,0:T(8,128)S(1)}, u32[]{:S(2)}, u32[]{:S(2)}) %collective-permute-start) | collective-permute-done | bytes 524320 | tf_op jit(solution)/shard_map/while/body/eval_jaxpr/ppermute | solution.py:14
  376.2 15.4 %collective-permute-done = f32[16,64,128]{2,1,0:T(8,128)S(1)} collective-permute-done((f32[16,64,128]{2,1,0:T(8,128)S(1)}, f32[16,64,128]{2,1,0:T(8,128)S(1)}, u32[]{:S(2)}, u32[]{:S(2)}) %collective-permute-start) | collective-permute-done | bytes 524320 | tf_op jit(solution)/shard_map/while/body/eval_jaxpr/ppermute | solution.py:14
  393.7 14.6 %collective-permute-done = f32[16,64,128]{2,1,0:T(8,128)S(1)} collective-permute-done((f32[16,64,128]{2,1,0:T(8,128)S(1)}, f32[16,64,128]{2,1,0:T(8,128)S(1)}, u32[]{:S(2)}, u32[]{:S(2)}) %collective-permute-start) | collective-permute-done | bytes 524320 | tf_op jit(solution)/shard_map/while/body/eval_jaxpr/ppermute | solution.py:14
  410.3 13.7 %collective-permute-done = f32[16,64,128]{2,1,0:T(8,128)S(1)} collective-permute-done((f32[16,64,128]{2,1,0:T(8,128)S(1)}, f32[16,64,128]{2,1,0:T(8,128)S(1)}, u32[]{:S(2)}, u32[]{:S(2)}) %collective-permute-start) | collective-permute-done | bytes 524320 | tf_op jit(solution)/shard_map/while/body/eval_jaxpr/ppermute | solution.py:14
  426.1 12.9 %collective-permute-done = f32[16,64,128]{2,1,0:T(8,128)S(1)} collective-permute-done((f32[16,64,128]{2,1,0:T(8,128)S(1)}, f32[16,64,128]{2,1,0:T(8,128)S(1)}, u32[]{:S(2)}, u32[]{:S(2)}) %collective-permute-start) | collective-permute-done | bytes 524320 | tf_op jit(solution)/shard_map/while/body/eval_jaxpr/ppermute | solution.py:14
  441.0 12.0 %collective-permute-done = f32[16,64,128]{2,1,0:T(8,128)S(1)} collective-permute-done((f32[16,64,128]{2,1,0:T(8,128)S(1)}, f32[16,64,128]{2,1,0:T(8,128)S(1)}, u32[]{:S(2)}, u32[]{:S(2)}) %collective-permute-start) | collective-permute-done | bytes 524320 | tf_op jit(solution)/shard_map/while/body/eval_jaxpr/ppermute | solution.py:14
  482.0 12.7 %collective-permute-done = f32[16,64,128]{2,1,0:T(8,128)S(1)} collective-permute-done((f32[16,64,128]{2,1,0:T(8,128)S(1)}, f32[16,64,128]{2,1,0:T(8,128)S(1)}, u32[]{:S(2)}, u32[]{:S(2)}) %collective-permute-start) | collective-permute-done | bytes 524320 | tf_op jit(solution)/shard_map/while/body/eval_jaxpr/ppermute | solution.py:14
  496.8 13.9 %collective-permute-done = f32[16,64,128]{2,1,0:T(8,128)S(1)} collective-permute-done((f32[16,64,128]{2,1,0:T(8,128)S(1)}, f32[16,64,128]{2,1,0:T(8,128)S(1)}, u32[]{:S(2)}, u32[]{:S(2)}) %collective-permute-start) | collective-permute-done | bytes 524320 | tf_op jit(solution)/shard_map/while/body/eval_jaxpr/ppermute | solution.py:14
  512.7 15.0 %collective-permute-done = f32[16,64,128]{2,1,0:T(8,128)S(1)} collective-permute-done((f32[16,64,128]{2,1,0:T(8,128)S(1)}, f32[16,64,128]{2,1,0:T(8,128)S(1)}, u32[]{:S(2)}, u32[]{:S(2)}) %collective-permute-start) | collective-permute-done | bytes 524320 | tf_op jit(solution)/shard_map/while/body/eval_jaxpr/ppermute | solution.py:14
  529.8 16.2 %collective-permute-done = f32[16,64,128]{2,1,0:T(8,128)S(1)} collective-permute-done((f32[16,64,128]{2,1,0:T(8,128)S(1)}, f32[16,64,128]{2,1,0:T(8,128)S(1)}, u32[]{:S(2)}, u32[]{:S(2)}) %collective-permute-start) | collective-permute-done | bytes 524320 | tf_op jit(solution)/shard_map/while/body/eval_jaxpr/ppermute | solution.py:14
  548.0 16.4 %collective-permute-done = f32[16,64,128]{2,1,0:T(8,128)S(1)} collective-permute-done((f32[16,64,128]{2,1,0:T(8,128)S(1)}, f32[16,64,128]{2,1,0:T(8,128)S(1)}, u32[]{:S(2)}, u32[]{:S(2)}) %collective-permute-start) | collective-permute-done | bytes 524320 | tf_op jit(solution)/shard_map/while/body/eval_jaxpr/ppermute | solution.py:14
  566.5 15.6 %collective-permute-done = f32[16,64,128]{2,1,0:T(8,128)S(1)} collective-permute-done((f32[16,64,128]{2,1,0:T(8,128)S(1)}, f32[16,64,128]{2,1,0:T(8,128)S(1)}, u32[]{:S(2)}, u32[]{:S(2)}) %collective-permute-start) | collective-permute-done | bytes 524320 | tf_op jit(solution)/shard_map/while/body/eval_jaxpr/ppermute | solution.py:14
  584.1 14.7 %collective-permute-done = f32[16,64,128]{2,1,0:T(8,128)S(1)} collective-permute-done((f32[16,64,128]{2,1,0:T(8,128)S(1)}, f32[16,64,128]{2,1,0:T(8,128)S(1)}, u32[]{:S(2)}, u32[]{:S(2)}) %collective-permute-start) | collective-permute-done | bytes 524320 | tf_op jit(solution)/shard_map/while/body/eval_jaxpr/ppermute | solution.py:14
  600.9 13.8 %collective-permute-done = f32[16,64,128]{2,1,0:T(8,128)S(1)} collective-permute-done((f32[16,64,128]{2,1,0:T(8,128)S(1)}, f32[16,64,128]{2,1,0:T(8,128)S(1)}, u32[]{:S(2)}, u32[]{:S(2)}) %collective-permute-start) | collective-permute-done | bytes 524320 | tf_op jit(solution)/shard_map/while/body/eval_jaxpr/ppermute | solution.py:14
  616.8 13.0 %collective-permute-done = f32[16,64,128]{2,1,0:T(8,128)S(1)} collective-permute-done((f32[16,64,128]{2,1,0:T(8,128)S(1)}, f32[16,64,128]{2,1,0:T(8,128)S(1)}, u32[]{:S(2)}, u32[]{:S(2)}) %collective-permute-start) | collective-permute-done | bytes 524320 | tf_op jit(solution)/shard_map/while/body/eval_jaxpr/ppermute | solution.py:14
  668.2 15.6 %copy.34 = bf16[12,256,16,64]{3,2,1,0:T(8,128)(2,1)} copy(bf16[12,256,16,64]{1,3,2,0:T(8,128)(2,1)} %add_convert_fusion) | data formatting | bytes 12582912 | tf_op jit(solution)/shard_map/reshape | solution.py:82
  683.8 17.2 %reshape.108 = bf16[3072,1024]{1,0:T(8,128)(2,1)} reshape(bf16[12,256,16,64]{3,2,1,0:T(8,128)(2,1)} %copy.34) | data formatting | bytes 12582912 | tf_op jit(solution)/shard_map/reshape | solution.py:82
  (220 shorter events, 270.0 us)
Async XLA Ops:
  6.5 40.2 %all-gather.2.cloned.1.call-start = ((), (), s32[]{:S(2)}) async-start(), calls=%async_computation | async-start | bytes 1769472 | tf_op jit(solution)/shard_map/all_gather | solution.py:42
  164.1 19.9 %collective-permute-start = (f32[16,64,128]{2,1,0:T(8,128)S(1)}, f32[16,64,128]{2,1,0:T(8,128)S(1)}, u32[]{:S(2)}, u32[]{:S(2)}) collective-permute-start(f32[16,64,128]{2,1,0:T(8,128)S(1)} %multiply_add_fusion.2), channel_id=1, source_target_pairs={{0,8},{8,16},{16,24},{24,32},{32,40},{40,48},{48,56},{56,64},{64,7... | collective-permute-start | bytes 1572872 | tf_op jit(solution)/shard_map/while/body/eval_jaxpr/ppermute | solution.py:14
  184.2 17.2 %collective-permute-start = (f32[16,64,128]{2,1,0:T(8,128)S(1)}, f32[16,64,128]{2,1,0:T(8,128)S(1)}, u32[]{:S(2)}, u32[]{:S(2)}) collective-permute-start(f32[16,64,128]{2,1,0:T(8,128)S(1)} %multiply_add_fusion.2), channel_id=1, source_target_pairs={{0,8},{8,16},{16,24},{24,32},{32,40},{40,48},{48,56},{56,64},{64,7... | collective-permute-start | bytes 1572872 | tf_op jit(solution)/shard_map/while/body/eval_jaxpr/ppermute | solution.py:14
  201.5 16.4 %collective-permute-start = (f32[16,64,128]{2,1,0:T(8,128)S(1)}, f32[16,64,128]{2,1,0:T(8,128)S(1)}, u32[]{:S(2)}, u32[]{:S(2)}) collective-permute-start(f32[16,64,128]{2,1,0:T(8,128)S(1)} %multiply_add_fusion.2), channel_id=1, source_target_pairs={{0,8},{8,16},{16,24},{24,32},{32,40},{40,48},{48,56},{56,64},{64,7... | collective-permute-start | bytes 1572872 | tf_op jit(solution)/shard_map/while/body/eval_jaxpr/ppermute | solution.py:14
  218.0 15.5 %collective-permute-start = (f32[16,64,128]{2,1,0:T(8,128)S(1)}, f32[16,64,128]{2,1,0:T(8,128)S(1)}, u32[]{:S(2)}, u32[]{:S(2)}) collective-permute-start(f32[16,64,128]{2,1,0:T(8,128)S(1)} %multiply_add_fusion.2), channel_id=1, source_target_pairs={{0,8},{8,16},{16,24},{24,32},{32,40},{40,48},{48,56},{56,64},{64,7... | collective-permute-start | bytes 1572872 | tf_op jit(solution)/shard_map/while/body/eval_jaxpr/ppermute | solution.py:14
  233.6 14.7 %collective-permute-start = (f32[16,64,128]{2,1,0:T(8,128)S(1)}, f32[16,64,128]{2,1,0:T(8,128)S(1)}, u32[]{:S(2)}, u32[]{:S(2)}) collective-permute-start(f32[16,64,128]{2,1,0:T(8,128)S(1)} %multiply_add_fusion.2), channel_id=1, source_target_pairs={{0,8},{8,16},{16,24},{24,32},{32,40},{40,48},{48,56},{56,64},{64,7... | collective-permute-start | bytes 1572872 | tf_op jit(solution)/shard_map/while/body/eval_jaxpr/ppermute | solution.py:14
  248.4 13.8 %collective-permute-start = (f32[16,64,128]{2,1,0:T(8,128)S(1)}, f32[16,64,128]{2,1,0:T(8,128)S(1)}, u32[]{:S(2)}, u32[]{:S(2)}) collective-permute-start(f32[16,64,128]{2,1,0:T(8,128)S(1)} %multiply_add_fusion.2), channel_id=1, source_target_pairs={{0,8},{8,16},{16,24},{24,32},{32,40},{40,48},{48,56},{56,64},{64,7... | collective-permute-start | bytes 1572872 | tf_op jit(solution)/shard_map/while/body/eval_jaxpr/ppermute | solution.py:14
  262.3 13.2 %collective-permute-start = (f32[16,64,128]{2,1,0:T(8,128)S(1)}, f32[16,64,128]{2,1,0:T(8,128)S(1)}, u32[]{:S(2)}, u32[]{:S(2)}) collective-permute-start(f32[16,64,128]{2,1,0:T(8,128)S(1)} %multiply_add_fusion.2), channel_id=1, source_target_pairs={{0,8},{8,16},{16,24},{24,32},{32,40},{40,48},{48,56},{56,64},{64,7... | collective-permute-start | bytes 1572872 | tf_op jit(solution)/shard_map/while/body/eval_jaxpr/ppermute | solution.py:14
  275.6 13.7 %collective-permute-start = (f32[16,64,128]{2,1,0:T(8,128)S(1)}, f32[16,64,128]{2,1,0:T(8,128)S(1)}, u32[]{:S(2)}, u32[]{:S(2)}) collective-permute-start(f32[16,64,128]{2,1,0:T(8,128)S(1)} %multiply_add_fusion.2), channel_id=1, source_target_pairs={{0,8},{8,16},{16,24},{24,32},{32,40},{40,48},{48,56},{56,64},{64,7... | collective-permute-start | bytes 1572872 | tf_op jit(solution)/shard_map/while/body/eval_jaxpr/ppermute | solution.py:14
  289.4 14.8 %collective-permute-start = (f32[16,64,128]{2,1,0:T(8,128)S(1)}, f32[16,64,128]{2,1,0:T(8,128)S(1)}, u32[]{:S(2)}, u32[]{:S(2)}) collective-permute-start(f32[16,64,128]{2,1,0:T(8,128)S(1)} %multiply_add_fusion.2), channel_id=1, source_target_pairs={{0,8},{8,16},{16,24},{24,32},{32,40},{40,48},{48,56},{56,64},{64,7... | collective-permute-start | bytes 1572872 | tf_op jit(solution)/shard_map/while/body/eval_jaxpr/ppermute | solution.py:14
  304.3 15.9 %collective-permute-start = (f32[16,64,128]{2,1,0:T(8,128)S(1)}, f32[16,64,128]{2,1,0:T(8,128)S(1)}, u32[]{:S(2)}, u32[]{:S(2)}) collective-permute-start(f32[16,64,128]{2,1,0:T(8,128)S(1)} %multiply_add_fusion.2), channel_id=1, source_target_pairs={{0,8},{8,16},{16,24},{24,32},{32,40},{40,48},{48,56},{56,64},{64,7... | collective-permute-start | bytes 1572872 | tf_op jit(solution)/shard_map/while/body/eval_jaxpr/ppermute | solution.py:14
  320.4 17.1 %collective-permute-start = (f32[16,64,128]{2,1,0:T(8,128)S(1)}, f32[16,64,128]{2,1,0:T(8,128)S(1)}, u32[]{:S(2)}, u32[]{:S(2)}) collective-permute-start(f32[16,64,128]{2,1,0:T(8,128)S(1)} %multiply_add_fusion.2), channel_id=1, source_target_pairs={{0,8},{8,16},{16,24},{24,32},{32,40},{40,48},{48,56},{56,64},{64,7... | collective-permute-start | bytes 1572872 | tf_op jit(solution)/shard_map/while/body/eval_jaxpr/ppermute | solution.py:14
  337.6 18.2 %collective-permute-start = (f32[16,64,128]{2,1,0:T(8,128)S(1)}, f32[16,64,128]{2,1,0:T(8,128)S(1)}, u32[]{:S(2)}, u32[]{:S(2)}) collective-permute-start(f32[16,64,128]{2,1,0:T(8,128)S(1)} %multiply_add_fusion.2), channel_id=1, source_target_pairs={{0,8},{8,16},{16,24},{24,32},{32,40},{40,48},{48,56},{56,64},{64,7... | collective-permute-start | bytes 1572872 | tf_op jit(solution)/shard_map/while/body/eval_jaxpr/ppermute | solution.py:14
  356.0 18.2 %collective-permute-start = (f32[16,64,128]{2,1,0:T(8,128)S(1)}, f32[16,64,128]{2,1,0:T(8,128)S(1)}, u32[]{:S(2)}, u32[]{:S(2)}) collective-permute-start(f32[16,64,128]{2,1,0:T(8,128)S(1)} %multiply_add_fusion.2), channel_id=1, source_target_pairs={{0,8},{8,16},{16,24},{24,32},{32,40},{40,48},{48,56},{56,64},{64,7... | collective-permute-start | bytes 1572872 | tf_op jit(solution)/shard_map/while/body/eval_jaxpr/ppermute | solution.py:14
  374.3 17.4 %collective-permute-start = (f32[16,64,128]{2,1,0:T(8,128)S(1)}, f32[16,64,128]{2,1,0:T(8,128)S(1)}, u32[]{:S(2)}, u32[]{:S(2)}) collective-permute-start(f32[16,64,128]{2,1,0:T(8,128)S(1)} %multiply_add_fusion.2), channel_id=1, source_target_pairs={{0,8},{8,16},{16,24},{24,32},{32,40},{40,48},{48,56},{56,64},{64,7... | collective-permute-start | bytes 1572872 | tf_op jit(solution)/shard_map/while/body/eval_jaxpr/ppermute | solution.py:14
  391.8 16.5 %collective-permute-start = (f32[16,64,128]{2,1,0:T(8,128)S(1)}, f32[16,64,128]{2,1,0:T(8,128)S(1)}, u32[]{:S(2)}, u32[]{:S(2)}) collective-permute-start(f32[16,64,128]{2,1,0:T(8,128)S(1)} %multiply_add_fusion.2), channel_id=1, source_target_pairs={{0,8},{8,16},{16,24},{24,32},{32,40},{40,48},{48,56},{56,64},{64,7... | collective-permute-start | bytes 1572872 | tf_op jit(solution)/shard_map/while/body/eval_jaxpr/ppermute | solution.py:14
  408.4 15.6 %collective-permute-start = (f32[16,64,128]{2,1,0:T(8,128)S(1)}, f32[16,64,128]{2,1,0:T(8,128)S(1)}, u32[]{:S(2)}, u32[]{:S(2)}) collective-permute-start(f32[16,64,128]{2,1,0:T(8,128)S(1)} %multiply_add_fusion.2), channel_id=1, source_target_pairs={{0,8},{8,16},{16,24},{24,32},{32,40},{40,48},{48,56},{56,64},{64,7... | collective-permute-start | bytes 1572872 | tf_op jit(solution)/shard_map/while/body/eval_jaxpr/ppermute | solution.py:14
  424.1 14.8 %collective-permute-start = (f32[16,64,128]{2,1,0:T(8,128)S(1)}, f32[16,64,128]{2,1,0:T(8,128)S(1)}, u32[]{:S(2)}, u32[]{:S(2)}) collective-permute-start(f32[16,64,128]{2,1,0:T(8,128)S(1)} %multiply_add_fusion.2), channel_id=1, source_target_pairs={{0,8},{8,16},{16,24},{24,32},{32,40},{40,48},{48,56},{56,64},{64,7... | collective-permute-start | bytes 1572872 | tf_op jit(solution)/shard_map/while/body/eval_jaxpr/ppermute | solution.py:14
  439.1 13.9 %collective-permute-start = (f32[16,64,128]{2,1,0:T(8,128)S(1)}, f32[16,64,128]{2,1,0:T(8,128)S(1)}, u32[]{:S(2)}, u32[]{:S(2)}) collective-permute-start(f32[16,64,128]{2,1,0:T(8,128)S(1)} %multiply_add_fusion.2), channel_id=1, source_target_pairs={{0,8},{8,16},{16,24},{24,32},{32,40},{40,48},{48,56},{56,64},{64,7... | collective-permute-start | bytes 1572872 | tf_op jit(solution)/shard_map/while/body/eval_jaxpr/ppermute | solution.py:14
  453.1 13.2 %collective-permute-start = (f32[16,64,128]{2,1,0:T(8,128)S(1)}, f32[16,64,128]{2,1,0:T(8,128)S(1)}, u32[]{:S(2)}, u32[]{:S(2)}) collective-permute-start(f32[16,64,128]{2,1,0:T(8,128)S(1)} %multiply_add_fusion.2), channel_id=1, source_target_pairs={{0,8},{8,16},{16,24},{24,32},{32,40},{40,48},{48,56},{56,64},{64,7... | collective-permute-start | bytes 1572872 | tf_op jit(solution)/shard_map/while/body/eval_jaxpr/ppermute | solution.py:14
  466.4 13.5 %collective-permute-start = (f32[16,64,128]{2,1,0:T(8,128)S(1)}, f32[16,64,128]{2,1,0:T(8,128)S(1)}, u32[]{:S(2)}, u32[]{:S(2)}) collective-permute-start(f32[16,64,128]{2,1,0:T(8,128)S(1)} %multiply_add_fusion.2), channel_id=1, source_target_pairs={{0,8},{8,16},{16,24},{24,32},{32,40},{40,48},{48,56},{56,64},{64,7... | collective-permute-start | bytes 1572872 | tf_op jit(solution)/shard_map/while/body/eval_jaxpr/ppermute | solution.py:14
  480.1 14.7 %collective-permute-start = (f32[16,64,128]{2,1,0:T(8,128)S(1)}, f32[16,64,128]{2,1,0:T(8,128)S(1)}, u32[]{:S(2)}, u32[]{:S(2)}) collective-permute-start(f32[16,64,128]{2,1,0:T(8,128)S(1)} %multiply_add_fusion.2), channel_id=1, source_target_pairs={{0,8},{8,16},{16,24},{24,32},{32,40},{40,48},{48,56},{56,64},{64,7... | collective-permute-start | bytes 1572872 | tf_op jit(solution)/shard_map/while/body/eval_jaxpr/ppermute | solution.py:14
  494.8 15.8 %collective-permute-start = (f32[16,64,128]{2,1,0:T(8,128)S(1)}, f32[16,64,128]{2,1,0:T(8,128)S(1)}, u32[]{:S(2)}, u32[]{:S(2)}) collective-permute-start(f32[16,64,128]{2,1,0:T(8,128)S(1)} %multiply_add_fusion.2), channel_id=1, source_target_pairs={{0,8},{8,16},{16,24},{24,32},{32,40},{40,48},{48,56},{56,64},{64,7... | collective-permute-start | bytes 1572872 | tf_op jit(solution)/shard_map/while/body/eval_jaxpr/ppermute | solution.py:14
  510.8 17.0 %collective-permute-start = (f32[16,64,128]{2,1,0:T(8,128)S(1)}, f32[16,64,128]{2,1,0:T(8,128)S(1)}, u32[]{:S(2)}, u32[]{:S(2)}) collective-permute-start(f32[16,64,128]{2,1,0:T(8,128)S(1)} %multiply_add_fusion.2), channel_id=1, source_target_pairs={{0,8},{8,16},{16,24},{24,32},{32,40},{40,48},{48,56},{56,64},{64,7... | collective-permute-start | bytes 1572872 | tf_op jit(solution)/shard_map/while/body/eval_jaxpr/ppermute | solution.py:14
  527.9 18.1 %collective-permute-start = (f32[16,64,128]{2,1,0:T(8,128)S(1)}, f32[16,64,128]{2,1,0:T(8,128)S(1)}, u32[]{:S(2)}, u32[]{:S(2)}) collective-permute-start(f32[16,64,128]{2,1,0:T(8,128)S(1)} %multiply_add_fusion.2), channel_id=1, source_target_pairs={{0,8},{8,16},{16,24},{24,32},{32,40},{40,48},{48,56},{56,64},{64,7... | collective-permute-start | bytes 1572872 | tf_op jit(solution)/shard_map/while/body/eval_jaxpr/ppermute | solution.py:14
  546.1 18.3 %collective-permute-start = (f32[16,64,128]{2,1,0:T(8,128)S(1)}, f32[16,64,128]{2,1,0:T(8,128)S(1)}, u32[]{:S(2)}, u32[]{:S(2)}) collective-permute-start(f32[16,64,128]{2,1,0:T(8,128)S(1)} %multiply_add_fusion.2), channel_id=1, source_target_pairs={{0,8},{8,16},{16,24},{24,32},{32,40},{40,48},{48,56},{56,64},{64,7... | collective-permute-start | bytes 1572872 | tf_op jit(solution)/shard_map/while/body/eval_jaxpr/ppermute | solution.py:14
  564.5 17.5 %collective-permute-start = (f32[16,64,128]{2,1,0:T(8,128)S(1)}, f32[16,64,128]{2,1,0:T(8,128)S(1)}, u32[]{:S(2)}, u32[]{:S(2)}) collective-permute-start(f32[16,64,128]{2,1,0:T(8,128)S(1)} %multiply_add_fusion.2), channel_id=1, source_target_pairs={{0,8},{8,16},{16,24},{24,32},{32,40},{40,48},{48,56},{56,64},{64,7... | collective-permute-start | bytes 1572872 | tf_op jit(solution)/shard_map/while/body/eval_jaxpr/ppermute | solution.py:14
  582.2 16.6 %collective-permute-start = (f32[16,64,128]{2,1,0:T(8,128)S(1)}, f32[16,64,128]{2,1,0:T(8,128)S(1)}, u32[]{:S(2)}, u32[]{:S(2)}) collective-permute-start(f32[16,64,128]{2,1,0:T(8,128)S(1)} %multiply_add_fusion.2), channel_id=1, source_target_pairs={{0,8},{8,16},{16,24},{24,32},{32,40},{40,48},{48,56},{56,64},{64,7... | collective-permute-start | bytes 1572872 | tf_op jit(solution)/shard_map/while/body/eval_jaxpr/ppermute | solution.py:14
  598.9 15.8 %collective-permute-start = (f32[16,64,128]{2,1,0:T(8,128)S(1)}, f32[16,64,128]{2,1,0:T(8,128)S(1)}, u32[]{:S(2)}, u32[]{:S(2)}) collective-permute-start(f32[16,64,128]{2,1,0:T(8,128)S(1)} %multiply_add_fusion.2), channel_id=1, source_target_pairs={{0,8},{8,16},{16,24},{24,32},{32,40},{40,48},{48,56},{56,64},{64,7... | collective-permute-start | bytes 1572872 | tf_op jit(solution)/shard_map/while/body/eval_jaxpr/ppermute | solution.py:14
  614.8 14.9 %collective-permute-start = (f32[16,64,128]{2,1,0:T(8,128)S(1)}, f32[16,64,128]{2,1,0:T(8,128)S(1)}, u32[]{:S(2)}, u32[]{:S(2)}) collective-permute-start(f32[16,64,128]{2,1,0:T(8,128)S(1)} %multiply_add_fusion.2), channel_id=1, source_target_pairs={{0,8},{8,16},{16,24},{24,32},{32,40},{40,48},{48,56},{56,64},{64,7... | collective-permute-start | bytes 1572872 | tf_op jit(solution)/shard_map/while/body/eval_jaxpr/ppermute | solution.py:14
  629.9 13.2 %collective-permute-start = (f32[16,64,128]{2,1,0:T(8,128)S(1)}, f32[16,64,128]{2,1,0:T(8,128)S(1)}, u32[]{:S(2)}, u32[]{:S(2)}) collective-permute-start(f32[16,64,128]{2,1,0:T(8,128)S(1)} %multiply_add_fusion.2), channel_id=1, source_target_pairs={{0,8},{8,16},{16,24},{24,32},{32,40},{40,48},{48,56},{56,64},{64,7... | collective-permute-start | bytes 1572872 | tf_op jit(solution)/shard_map/while/body/eval_jaxpr/ppermute | solution.py:14
  643.2 13.2 %collective-permute-start = (f32[16,64,128]{2,1,0:T(8,128)S(1)}, f32[16,64,128]{2,1,0:T(8,128)S(1)}, u32[]{:S(2)}, u32[]{:S(2)}) collective-permute-start(f32[16,64,128]{2,1,0:T(8,128)S(1)} %multiply_add_fusion.2), channel_id=1, source_target_pairs={{0,8},{8,16},{16,24},{24,32},{32,40},{40,48},{48,56},{56,64},{64,7... | collective-permute-start | bytes 1572872 | tf_op jit(solution)/shard_map/while/body/eval_jaxpr/ppermute | solution.py:14
  (3 other events, 523.2 us)
Sparse Core Ops, SparseCore 0:
  9.2 27.9 all-gather.1
where the time goes:
time: 712 us; the launch traced here: 708 us
  waiting for transfers between devices  428 us (60%)
  local copies, waits for them, and re-layouts  89.5 us (13%)
  matrix products  84.1 us (12%)
  starting transfers between devices  61.4 us (9%)
  other arithmetic  30.6 us (4%)
  between operations  13.5 us (2%)
    ppermute x31, waiting for transfers between devices, passed_along(): lax.ppermute(value, axis, [(source, source + steps) for source in range(i...  427 us
    ppermute x31, starting transfers between devices, passed_along(): lax.ppermute(value, axis, [(source, source + steps) for source in range(i...  61.4 us
    dot_general x12, matrix products, group_terms(): jnp.einsum('hts,shp->thp', weights, inputs, preferred_element_type=jnp.fl...  41.6 us
    reshape x2, local copies, waits for them, and re-layouts, shards(): return output.reshape(group_count * GROUP, heads_here * HEAD_DIM)  32.8 us
    reshape x2, local copies, waits for them, and re-layouts, shards(): inputs = frames.reshape(group_count, GROUP, heads_here, HEAD_DIM)[inverse]  31.8 us
    dot_general x12, matrix products, group_terms(): jnp.einsum('shp,ns->hpn', carried, input_map, preferred_element_type=jnp....  26 us
  transfers between devices with their start and end apart: 32, of which 31 were waited for; matrix products, arithmetic and copies ran while one was open for 6% of the time, Pallas kernels for 0%

commit v1 on v0

v1 whole, which is shorter than its diff:
```python
import functools

import jax
import jax.numpy as jnp
from jax import lax
from jax.experimental import pallas as pl
from jax.experimental.pallas import tpu as pltpu
from jax.sharding import PartitionSpec as P

HEADS = 16
HEAD_DIM = 64
WIDTH = HEADS * HEAD_DIM
STATE = 128
GROUP = 256
CHUNK = 128
SLOTS = 12
CHUNKS = SLOTS * GROUP // CHUNK
FRAMES = SLOTS * GROUP
SHARD = 32
OWNERS = 32
EXTRA = 16
F32, BF16 = jnp.float32, jnp.bfloat16
VMEM_SPEC = pl.BlockSpec(memory_space=pltpu.VMEM)


def split(value, parts):
    out = []
    for _ in range(parts):
        piece = value.astype(BF16)
        out.append(piece)
        value = value - piece.astype(F32)
    return out


def over_heads(value, hot):
    return lax.dot_general(value, hot, (((0,), (0,)), ((), ())), preferred_element_type=F32)


def slot_of(c, pos_ref):
    slot = 0
    for i in range(SLOTS):
        slot = slot + jnp.where(lax.rem(pos_ref[i], SLOTS) == c, i, 0)
    return slot


def block_of_slice(j):
    return slice((j // 8) * 32, (j // 8) * 32 + 32), slice((j % 8) * 128, (j % 8) * 128 + 128)


def summary_kernel(
    pos_ref, place_ref, x_ref, ld_ref, skip_ref, *rest
):
    pieces = rest[:8]
    pay_ref, proj_ref, eg_ref, rows_ref, acc_ref, w_ref, hot_ref, r_ref = rest[8:]
    step = pl.program_id(0)

    @pl.when(step == 0)
    def _():
        head_of_lane = lax.shift_right_logical(lax.broadcasted_iota(jnp.int32, (2 * HEADS, WIDTH), 1), 6)
        row = lax.broadcasted_iota(jnp.int32, (2 * HEADS, WIDTH), 0) & (HEADS - 1)
        hot_ref[...] = jnp.where(head_of_lane == row, 1.0, 0.0).astype(BF16)
        acc_ref[...] = jnp.zeros_like(acc_ref)
        slots = [slot_of(c, pos_ref) for c in range(SLOTS)]
        for i in range(8):
            at = pl.ds(pl.multiple_of(place_ref[i] * SHARD, SHARD), SHARD)
            for c in range(SLOTS):
                lanes = pl.ds(pl.multiple_of(slots[c] * GROUP, GROUP), GROUP)
                proj_ref[at, c * GROUP : (c + 1) * GROUP] = pieces[i][:, lanes]
        for c in range(SLOTS):
            for half in range(2):
                lanes = pl.ds(pl.multiple_of(slots[c] * GROUP + half * CHUNK, CHUNK), CHUNK)
                r_ref[(2 * c + half) * HEADS : (2 * c + half + 1) * HEADS, :] = ld_ref[:, lanes]
        upto = lax.broadcasted_iota(jnp.int32, (CHUNK, CHUNK), 0) <= lax.broadcasted_iota(
            jnp.int32, (CHUNK, CHUNK), 1
        )
        r_ref[...] = jnp.dot(
            r_ref[...], jnp.where(upto, 1.0, 0.0), precision=lax.Precision.HIGHEST, preferred_element_type=F32
        )
        lane = lax.broadcasted_iota(jnp.int32, (HEADS, CHUNK), 1)
        alpha = jnp.zeros((HEADS, CHUNK), F32)
        past = jnp.zeros((HEADS, 1), F32)
        for c in range(CHUNKS):
            r = r_ref[c * HEADS : (c + 1) * HEADS, :]
            pivot = r[:, CHUNK // 2 - 1 : CHUNK // 2]
            alpha = jnp.where(lane == c, pivot + past, alpha)
            past = r[:, CHUNK - 1 :] - pivot
            for k, part in enumerate(split(jnp.exp(pivot - r), 2)):
                eg_ref[c, k * HEADS : (k + 1) * HEADS, :CHUNK] = part
            for k, part in enumerate(split(jnp.exp(r - pivot), 2)):
                eg_ref[c, k * HEADS : (k + 1) * HEADS, CHUNK:] = part
        hot = hot_ref[...]
        rows = over_heads(jnp.concatenate(split(jnp.exp(alpha), 2)), hot)
        rows_ref[:CHUNKS, :] = rows[:CHUNKS, :]
        skip = sum(
            jnp.dot(jnp.broadcast_to(part.astype(F32), (8, HEADS)).astype(BF16), hot[:HEADS], preferred_element_type=F32)
            for part in split(skip_ref[...], 3)
        )
        rows_ref[CHUNKS:, :] = skip
        after = jnp.zeros((HEADS, 1), F32)
        for c in reversed(range(CHUNKS)):
            r = r_ref[c * HEADS : (c + 1) * HEADS, :]
            last = r[:, CHUNK - 1 :]
            for k, part in enumerate(split(jnp.exp((last - r) + after), 2)):
                w_ref[c // 2, k * HEADS : (k + 1) * HEADS, (c % 2) * CHUNK : (c % 2 + 1) * CHUNK] = part
            after = after + last
        decay = jnp.zeros((HEADS, CHUNK), F32)
        for k, part in enumerate(split(jnp.exp(after), 3)):
            decay = jnp.where(lane == k, part.astype(F32), decay)
        decay = over_heads(decay.astype(BF16), hot[:HEADS])[:EXTRA].astype(BF16)
        for j in range(OWNERS):
            pay_ref[j, 32:, :] = decay[:, block_of_slice(j)[1]]

    weight = over_heads(w_ref[step], hot_ref[...])
    scaled = (x_ref[...].astype(F32) * weight).astype(BF16)
    lanes = pl.ds(pl.multiple_of(step * GROUP, GROUP), GROUP)
    acc_ref[...] += jnp.dot(proj_ref[:STATE, lanes], scaled, preferred_element_type=F32)

    @pl.when(step == SLOTS - 1)
    def _():
        for j in range(OWNERS):
            pay_ref[j, :32, :] = acc_ref[block_of_slice(j)].astype(BF16)


def prefix_kernel(in_ref, out_ref):
    carry = jnp.zeros((32, 128), F32)
    for d in range(OWNERS):
        out_ref[d] = carry.astype(BF16)
        decay = in_ref[d, 32:48, :].astype(F32)
        decay = decay[0:1] + decay[1:2] + decay[2:3]
        carry = decay * carry + in_ref[d, :32, :].astype(F32)


def mix_kernel(pos_ref, x_ref, proj_ref, eg_ref, rows_ref, carry_ref, out_ref, held_ref, hot_ref, lhs_ref, rhs_ref):
    step = pl.program_id(0)

    @pl.when(step == 0)
    def _():
        head_of_lane = lax.shift_right_logical(lax.broadcasted_iota(jnp.int32, (2 * HEADS, WIDTH), 1), 6)
        row = lax.broadcasted_iota(jnp.int32, (2 * HEADS, WIDTH), 0) & (HEADS - 1)
        hot_ref[...] = jnp.where(head_of_lane == row, 1.0, 0.0).astype(BF16)
        lhs_ref[CHUNK:, STATE:] = jnp.zeros((STATE, STATE), BF16)
        for j in range(OWNERS):
            held_ref[block_of_slice(j)] = carry_ref[j].astype(F32)

    causal = lax.broadcasted_iota(jnp.int32, (CHUNK, CHUNK), 0) >= lax.broadcasted_iota(
        jnp.int32, (CHUNK, CHUNK), 1
    )
    skip = rows_ref[CHUNKS : CHUNKS + 1, :]
    for half in range(2):
        frames = slice(half * CHUNK, (half + 1) * CHUNK)
        b = proj_ref[:STATE, frames]
        c_t = proj_ref[STATE:, frames].T
        coupling = jnp.dot(c_t, b, preferred_element_type=F32)
        lhs_ref[:CHUNK, :CHUNK] = jnp.where(causal, coupling, 0.0).astype(BF16)
        lhs_ref[:CHUNK, CHUNK:] = c_t
        lhs_ref[CHUNK:, :CHUNK] = b
        held = held_ref[...] * rows_ref[pl.ds(2 * step + half, 1), :]
        scale = over_heads(eg_ref[half], hot_ref[...])
        x = x_ref[frames, :].astype(F32)
        rhs_ref[:CHUNK, :] = (x * scale[:CHUNK]).astype(BF16)
        rhs_ref[CHUNK:, :] = held.astype(BF16)
        both = jnp.dot(lhs_ref[...], rhs_ref[...], preferred_element_type=F32)
        out_ref[frames, :] = (both[:CHUNK] * scale[CHUNK:] + skip * x).astype(BF16)
        held_ref[...] = held + both[CHUNK:]


def shards(frames, state_proj, log_decay, skip_gain, group_pos):
    def permuted(value, steps):
        return lax.ppermute(value, "head", [(i, (i + steps) % 8) for i in range(8)])

    def partner(value):
        return lax.ppermute(value, "head", [(i, i ^ 1) for i in range(8)])

    near = [state_proj] + [permuted(state_proj, 2 * k) for k in (1, 3, 2)]
    pieces = near + [partner(piece) for piece in near]
    me = lax.axis_index("head")
    hops = jnp.array([0, 2, 6, 4], jnp.int32)
    from_ = lax.rem(me + 8 - hops, 8)
    place = jnp.concatenate([from_, from_ ^ 1])

    def x_index(c, pos_ref, *_):
        return (slot_of(c, pos_ref), 0)

    pay, proj, eg, rows = pl.pallas_call(
        summary_kernel,
        grid_spec=pltpu.PrefetchScalarGridSpec(
            num_scalar_prefetch=2,
            grid=(SLOTS,),
            in_specs=[pl.BlockSpec((GROUP, WIDTH), x_index)] + [VMEM_SPEC] * 10,
            out_specs=[VMEM_SPEC] * 4,
            scratch_shapes=[
                pltpu.VMEM((STATE, WIDTH), F32),
                pltpu.VMEM((SLOTS, 2 * HEADS, GROUP), BF16),
                pltpu.VMEM((2 * HEADS, WIDTH), BF16),
                pltpu.VMEM((CHUNKS * HEADS, CHUNK), F32),
            ],
        ),
        out_shape=[
            jax.ShapeDtypeStruct((OWNERS, 32 + EXTRA, 128), BF16),
            jax.ShapeDtypeStruct((2 * STATE, FRAMES), BF16),
            jax.ShapeDtypeStruct((CHUNKS, 2 * HEADS, GROUP), BF16),
            jax.ShapeDtypeStruct((CHUNKS + 8, WIDTH), F32),
        ],
        name="summary",
    )(group_pos, place, frames, log_decay, skip_gain.reshape(1, HEADS), *pieces)
    pay = lax.all_to_all(pay, "seq", 0, 0, tiled=True)
    carry = pl.pallas_call(
        prefix_kernel,
        in_specs=[VMEM_SPEC],
        out_specs=VMEM_SPEC,
        out_shape=jax.ShapeDtypeStruct((OWNERS, 32, 128), BF16),
        name="prefix",
    )(pay)
    carry = lax.all_to_all(carry, "seq", 0, 0, tiled=True)
    return pl.pallas_call(
        mix_kernel,
        grid_spec=pltpu.PrefetchScalarGridSpec(
            num_scalar_prefetch=1,
            grid=(SLOTS,),
            in_specs=[
                pl.BlockSpec((GROUP, WIDTH), x_index),
                pl.BlockSpec((2 * STATE, GROUP), lambda c, *_: (0, c)),
                pl.BlockSpec((2, 2 * HEADS, GROUP), lambda c, *_: (c, 0, 0)),
                VMEM_SPEC,
                VMEM_SPEC,
            ],
            out_specs=pl.BlockSpec((GROUP, WIDTH), lambda c, *_: (c, 0)),
            scratch_shapes=[
                pltpu.VMEM((STATE, WIDTH), F32),
                pltpu.VMEM((2 * HEADS, WIDTH), BF16),
                pltpu.VMEM((CHUNK + STATE, CHUNK + STATE), BF16),
                pltpu.VMEM((CHUNK + STATE, WIDTH), BF16),
            ],
        ),
        out_shape=jax.ShapeDtypeStruct((FRAMES, WIDTH), BF16),
        name="mix",
    )(group_pos, frames, proj, eg, rows, carry)


def solution(mesh):
    return jax.shard_map(
        shards,
        mesh=mesh,
        in_specs=(P("seq", "head"), P("head", "seq"), P("head", "seq"), P("head"), P("seq")),
        out_specs=P("seq", "head"),
        check_vma=False,
    )
```

time: 712 us -> 91.9 us (0.13)
  the two profiles are of different devices: /device:TPU:30 before, /device:TPU:4 now
where the time goes in v1:
time: 91.9 us; the launch traced here: 91.1 us
  blocking collectives  44.3 us (48%)
  Pallas kernels  31.9 us (35%)
  waiting for transfers between devices  8.34 us (9%)
  starting transfers between devices  4.26 us (5%)
  other arithmetic  1.36 us (1%)
    all_to_all x1, blocking collectives, shards(): pay = lax.all_to_all(pay, 'seq', 0, 0, tiled=True)  26.3 us
    all_to_all x1, blocking collectives, shards(): carry = lax.all_to_all(carry, 'seq', 0, 0, tiled=True)  18.1 us
    pallas_call x1, Pallas kernels, shards(): pl.pallas_call(mix_kernel, grid_spec=pltpu.PrefetchScalarGridSpec(num_sca...  15.4 us
    pallas_call x1, Pallas kernels, shards(): pl.pallas_call(summary_kernel, grid_spec=pltpu.PrefetchScalarGridSpec(num...  14.7 us
    ppermute x3, waiting for transfers between devices, permuted(): return lax.ppermute(value, 'head', [(i, (i + steps) % 8) for i in range(8)])  8.31 us
    ppermute x3, starting transfers between devices, permuted(): return lax.ppermute(value, 'head', [(i, (i + steps) % 8) for i in range(8)])  4.24 us
  transfers between devices with their start and end apart: 7, of which 3 were waited for; matrix products, arithmetic and copies ran while one was open for 1% of the time, Pallas kernels for 0%

profile of v1, /device:TPU:4, one launch (start us, length us, event | category | flops | bytes accessed | tf_op | source)
XLA Modules:
  0.0 91.1 jit_solution(3019322518794952356)
XLA Ops:
  0.0 2.2 %collective-permute-start.2 = (bf16[32,3072]{1,0:T(8,128)(2,1)}, bf16[32,3072]{1,0:T(8,128)(2,1)S(1)}, u32[]{:S(2)}, u32[]{:S(2)}) collective-permute-start(bf16[32,3072]{1,0:T(8,128)(2,1)} %rest_0_.1), channel_id=1, source_target_pairs={{0,4},{1,5},{2,6},{3,7},{4,0},{5,1},{6,2},{7,3},{8,12},{9,13},{10,... | collective-permute-start | bytes 589832 | tf_op jit(solution)/shard_map/ppermute | solution.py:169
  2.2 0.4 collective-permute-start.1
  2.7 1.6 %collective-permute-start = (bf16[32,3072]{1,0:T(8,128)(2,1)}, bf16[32,3072]{1,0:T(8,128)(2,1)S(1)}, u32[]{:S(2)}, u32[]{:S(2)}) collective-permute-start(bf16[32,3072]{1,0:T(8,128)(2,1)} %rest_0_.1), channel_id=1, source_target_pairs={{0,2},{1,3},{2,4},{3,5},{4,6},{5,7},{6,0},{7,1},{8,10},{9,11},{10,... | collective-permute-start | bytes 589832 | tf_op jit(solution)/shard_map/ppermute | solution.py:169
  4.2 0.0 collective-permute-start.3
  4.2 5.3 %collective-permute-done.2.rest_3_ = bf16[32,3072]{1,0:T(8,128)(2,1)S(1)} collective-permute-done((bf16[32,3072]{1,0:T(8,128)(2,1)}, bf16[32,3072]{1,0:T(8,128)(2,1)S(1)}, u32[]{:S(2)}, u32[]{:S(2)}) %collective-permute-start.2) | collective-permute-done | bytes 196640 | tf_op jit(solution)/shard_map/ppermute | solution.py:169
  9.5 0.0 copy-start
  9.5 0.0 collective-permute-start.6
  9.5 2.1 %collective-permute-done.1.rest_2_ = bf16[32,3072]{1,0:T(8,128)(2,1)S(1)} collective-permute-done((bf16[32,3072]{1,0:T(8,128)(2,1)}, bf16[32,3072]{1,0:T(8,128)(2,1)S(1)}, u32[]{:S(2)}, u32[]{:S(2)}) %collective-permute-start.1) | collective-permute-done | bytes 196640 | tf_op jit(solution)/shard_map/ppermute | solution.py:169
  11.7 0.0 copy-start.1
  11.7 0.0 collective-permute-start.5
  11.7 0.9 collective-permute-done.rest_1_
  12.6 0.0 collective-permute-start.4
  12.6 0.7 broadcast_xor_fusion
  13.3 0.7 pad_add_fusion.place_ref
  14.0 0.0 collective-permute-done.3.rest_4_
  14.0 0.0 collective-permute-done.6.rest_7_
  14.0 0.0 copy-start.4
  14.0 0.0 collective-permute-done.5.rest_6_
  14.0 0.0 copy-start.5
  14.0 0.0 collective-permute-done.4.rest_5_
  14.0 0.0 copy-done
  14.0 0.0 copy-done.1
  14.0 0.0 copy-done.2
  14.0 0.6 copy-done.3
  14.6 0.1 copy-done.4
  14.7 0.1 copy-done.5
  14.8 0.1 copy-done.6
  14.9 14.7 %summary.1 = (bf16[32,48,128]{2,1,0:T(8,128)(2,1)}, bf16[256,3072]{1,0:T(8,128)(2,1)}, bf16[24,32,256]{2,1,0:T(8,128)(2,1)}, f32[32,1024]{1,0:T(8,128)}) custom-call(s32[12]{0:T(128)} %pos_ref.3, s32[8]{0:T(128)} %pad_add_fusion.place_ref, bf16[3072,1024]{1,0:T(8,128)(2,1)} %x_ref.3, f32[16,3072]{1,0:T(8,128)} %ld_ref.1, f32[1,16]{1,0:T(1,128)} %bitcast.1, ...), custom_call_target="tpu_custom_call" | custom-call | tf_op jit(solution)/shard_map/summary/pallas_call | solution.py:184
  29.6 26.3 %all_to_all.10.in_ref = bf16[32,48,128]{2,1,0:T(8,128)(2,1)} all-to-all(bf16[32,48,128]{2,1,0:T(8,128)(2,1)} %get-tuple-element.12), channel_id=1, replica_groups=mesh['seq'=32,'head'=8] {'seq'}, dimensions={0} | all-to-all | bytes 786432 | tf_op jit(solution)/shard_map/all_to_all | solution.py:206
  55.9 1.8 %prefix.1 = bf16[32,32,128]{2,1,0:T(8,128)(2,1)} custom-call(bf16[32,48,128]{2,1,0:T(8,128)(2,1)} %all_to_all.10.in_ref), custom_call_target="tpu_custom_call" | custom-call | tf_op jit(solution)/shard_map/prefix/pallas_call | solution.py:207
  57.6 18.1 %all_to_all.11.carry_ref = bf16[32,32,128]{2,1,0:T(8,128)(2,1)} all-to-all(bf16[32,32,128]{2,1,0:T(8,128)(2,1)} %prefix.1), channel_id=1, replica_groups=mesh['seq'=32,'head'=8] {'seq'}, dimensions={0} | all-to-all | bytes 524288 | tf_op jit(solution)/shard_map/all_to_all | solution.py:214
  75.7 15.4 %mix.1 = bf16[3072,1024]{1,0:T(8,128)(2,1)} custom-call(s32[12]{0:T(128)} %pos_ref.3, bf16[3072,1024]{1,0:T(8,128)(2,1)} %x_ref.3, bf16[256,3072]{1,0:T(8,128)(2,1)} %get-tuple-element.9.proj_ref, bf16[24,32,256]{2,1,0:T(8,128)(2,1)} %get-tuple-element.10.eg_ref, f32[32,1024]{1,0:T(8,128)} %get-tuple-element.11.rows_ref, ...), custom_call_target="tpu_custom_call" | custom-call | tf_op jit(solution)/shard_map/mix/pallas_call | solution.py:215
  (3 shorter events, 0.0 us)
Async XLA Ops:
  0.0 9.5 %collective-permute-start.2 = (bf16[32,3072]{1,0:T(8,128)(2,1)}, bf16[32,3072]{1,0:T(8,128)(2,1)S(1)}, u32[]{:S(2)}, u32[]{:S(2)}) collective-permute-start(bf16[32,3072]{1,0:T(8,128)(2,1)} %rest_0_.1), channel_id=1, source_target_pairs={{0,4},{1,5},{2,6},{3,7},{4,0},{5,1},{6,2},{7,3},{8,12},{9,13},{10,... | collective-permute-start | bytes 589832 | tf_op jit(solution)/shard_map/ppermute | solution.py:169
  2.2 9.5 %collective-permute-start.1 = (bf16[32,3072]{1,0:T(8,128)(2,1)}, bf16[32,3072]{1,0:T(8,128)(2,1)S(1)}, u32[]{:S(2)}, u32[]{:S(2)}) collective-permute-start(bf16[32,3072]{1,0:T(8,128)(2,1)} %rest_0_.1), channel_id=1, source_target_pairs={{0,6},{1,7},{2,0},{3,1},{4,2},{5,3},{6,4},{7,5},{8,14},{9,15},{10,... | collective-permute-start | bytes 589832 | tf_op jit(solution)/shard_map/ppermute | solution.py:169
  2.7 9.9 %collective-permute-start = (bf16[32,3072]{1,0:T(8,128)(2,1)}, bf16[32,3072]{1,0:T(8,128)(2,1)S(1)}, u32[]{:S(2)}, u32[]{:S(2)}) collective-permute-start(bf16[32,3072]{1,0:T(8,128)(2,1)} %rest_0_.1), channel_id=1, source_target_pairs={{0,2},{1,3},{2,4},{3,5},{4,6},{5,7},{6,0},{7,1},{8,10},{9,11},{10,... | collective-permute-start | bytes 589832 | tf_op jit(solution)/shard_map/ppermute | solution.py:169
  4.2 9.7 %collective-permute-start.3 = (bf16[32,3072]{1,0:T(8,128)(2,1)}, bf16[32,3072]{1,0:T(8,128)(2,1)S(1)}, u32[]{:S(2)}, u32[]{:S(2)}) collective-permute-start(bf16[32,3072]{1,0:T(8,128)(2,1)} %rest_0_.1), channel_id=1, source_target_pairs={{0,1},{1,0},{2,3},{3,2},{4,5},{5,4},{6,7},{7,6},{8,9},{9,8},{10,11... | collective-permute-start | bytes 589832 | tf_op jit(solution)/shard_map/ppermute | solution.py:172
  9.5 4.5 %copy-start = (bf16[32,3072]{1,0:T(8,128)(2,1)}, bf16[32,3072]{1,0:T(8,128)(2,1)S(1)}, u32[]{:S(2)}) copy-start(bf16[32,3072]{1,0:T(8,128)(2,1)S(1)} %collective-permute-done.2.rest_3_) | copy-start | bytes 589828
  9.5 4.4 %collective-permute-start.6 = (bf16[32,3072]{1,0:T(8,128)(2,1)S(1)}, bf16[32,3072]{1,0:T(8,128)(2,1)S(1)}, u32[]{:S(2)}, u32[]{:S(2)}) collective-permute-start(bf16[32,3072]{1,0:T(8,128)(2,1)S(1)} %collective-permute-done.2.rest_3_), channel_id=1, source_target_pairs={{0,1},{1,0},{2,3},{3,2},{4,5},{5,4},{6,7},{7,6},{8,9},{9,8},{10,11... | collective-permute-start | bytes 589832 | tf_op jit(solution)/shard_map/ppermute | solution.py:172
  11.7 2.3 %copy-start.1 = (bf16[32,3072]{1,0:T(8,128)(2,1)}, bf16[32,3072]{1,0:T(8,128)(2,1)S(1)}, u32[]{:S(2)}) copy-start(bf16[32,3072]{1,0:T(8,128)(2,1)S(1)} %collective-permute-done.1.rest_2_) | copy-start | bytes 589828
  11.7 2.3 %collective-permute-start.5 = (bf16[32,3072]{1,0:T(8,128)(2,1)S(1)}, bf16[32,3072]{1,0:T(8,128)(2,1)S(1)}, u32[]{:S(2)}, u32[]{:S(2)}) collective-permute-start(bf16[32,3072]{1,0:T(8,128)(2,1)S(1)} %collective-permute-done.1.rest_2_), channel_id=1, source_target_pairs={{0,1},{1,0},{2,3},{3,2},{4,5},{5,4},{6,7},{7,6},{8,9},{9,8},{10,11... | collective-permute-start | bytes 589832 | tf_op jit(solution)/shard_map/ppermute | solution.py:172
  12.6 1.5 %copy-start.2 = (bf16[32,3072]{1,0:T(8,128)(2,1)}, bf16[32,3072]{1,0:T(8,128)(2,1)S(1)}, u32[]{:S(2)}) copy-start(bf16[32,3072]{1,0:T(8,128)(2,1)S(1)} %collective-permute-done.rest_1_) | copy-start | bytes 589828
  12.6 1.4 %collective-permute-start.4 = (bf16[32,3072]{1,0:T(8,128)(2,1)S(1)}, bf16[32,3072]{1,0:T(8,128)(2,1)S(1)}, u32[]{:S(2)}, u32[]{:S(2)}) collective-permute-start(bf16[32,3072]{1,0:T(8,128)(2,1)S(1)} %collective-permute-done.rest_1_), channel_id=1, source_target_pairs={{0,1},{1,0},{2,3},{3,2},{4,5},{5,4},{6,7},{7,6},{8,9},{9,8},{10,11... | collective-permute-start | bytes 589832 | tf_op jit(solution)/shard_map/ppermute | solution.py:172
  14.0 0.7 copy-start.3
  14.0 0.8 copy-start.4
  14.0 0.8 copy-start.5
  14.0 0.8 copy-start.6

commit v2 on v0

v2 whole, which is shorter than its diff:
```python
import functools

import jax
import jax.numpy as jnp
from jax import lax
from jax.experimental import pallas as pl
from jax.experimental.pallas import tpu as pltpu
from jax.sharding import PartitionSpec as P

HEADS = 16
HEAD_DIM = 64
WIDTH = HEADS * HEAD_DIM
STATE = 128
GROUP = 256
CHUNK = 128
SLOTS = 12
CHUNKS = SLOTS * GROUP // CHUNK
FRAMES = SLOTS * GROUP
COLS = CHUNKS * HEADS
SHARD = 32
OWNERS = 32
EXTRA = 8
DECAY_VMEM = 58
WIDE_VMEM = 58
MID_VMEM = 58
WIDE = 256
SPANS = 4
SPAN = FRAMES // SPANS
F32, BF16 = jnp.float32, jnp.bfloat16
VMEM_SPEC = pl.BlockSpec(memory_space=pltpu.VMEM)


def iota(shape, axis):
    return lax.broadcasted_iota(jnp.int32, shape, axis)


def exact_dot(a, b, dims=(((1,), (0,)), ((), ()))):
    return lax.dot_general(a, b, dims, precision=lax.Precision.HIGHEST, preferred_element_type=F32)


def split(value, parts):
    out = []
    for _ in range(parts):
        piece = value.astype(BF16)
        out.append(piece)
        value = value - piece.astype(F32)
    return out


def over_lanes(source, chunk, start, width):
    rows = source.shape[0]
    base = lax.rem(chunk, 8) * HEADS
    head = lax.shift_right_logical(iota((rows, 128), 1), 6)
    return jnp.concatenate(
        [jnp.take_along_axis(source, head + (base + at // HEAD_DIM), axis=1) for at in range(start, start + width, 128)],
        axis=1,
    )


def column_of(chunk):
    return pl.ds(pl.multiple_of((chunk // 8) * 128, 128), 128)


def block_of_slice(j):
    return slice((j // 8) * 32, (j // 8) * 32 + 32), slice((j % 8) * 128, (j % 8) * 128 + 128)


def tile_of(chunk):
    return pl.ds(pl.multiple_of((chunk // 8) * 256, 256), 256)


def heads_of(hot_ref, chunk):
    rows = hot_ref[pl.ds(pl.multiple_of(112 - lax.rem(chunk, 8) * HEADS, HEADS), 128), :]
    return jnp.concatenate([rows, rows], axis=0)


def fill_hot(hot_ref):
    head = iota((256, WIDTH), 0) - 112
    hot_ref[...] = jnp.where(head == lax.shift_right_logical(iota((256, WIDTH), 1), 6), 1.0, 0.0).astype(BF16)


def store_pair(ref, value):
    for k, part in enumerate(split(value, 2)):
        for block in range(COLS // 128):
            ref[:, block * 256 + k * 128 : block * 256 + (k + 1) * 128] = part[:, block * 128 : (block + 1) * 128]


def decay_kernel(
    pos_ref, x_ref, ld_ref, skip_ref,
    slot_ref, scaled_ref, in_ref, out_ref, far_ref, far_pair_ref, total_ref,
    hot_ref, log_ref, w_ref, w_pair_ref, x_all, scaled_all, sems, out_sems,
):
    def fetch(i):
        return pltpu.make_async_copy(x_ref.at[pl.ds(i * GROUP, GROUP), :], x_all.at[i], sems.at[i])

    def put(i):
        return pltpu.make_async_copy(scaled_all.at[i], scaled_ref.at[pl.ds(i * GROUP, GROUP), :], out_sems.at[i])

    for i in range(SLOTS):
        fetch(i).start()
    base = pos_ref[0] - lax.rem(pos_ref[0], SLOTS)
    for i in range(SLOTS):
        place = pos_ref[i] - base
        slot_ref[place] = i
        for half in range(2):
            at = pl.ds(pl.multiple_of((2 * place + half) * HEADS, HEADS), HEADS)
            log_ref[at, :] = ld_ref[:, i * GROUP + half * CHUNK : i * GROUP + (half + 1) * CHUNK]
    upto = iota((CHUNK, CHUNK), 1) <= iota((CHUNK, CHUNK), 0)
    upto = jnp.where(upto, 1.0, 0.0).astype(BF16)
    r = sum(
        lax.dot_general(upto, part, (((1,), (1,)), ((), ())), preferred_element_type=F32)
        for part in split(log_ref[...], 3)
    )
    pivot = r[CHUNK // 2 - 1 : CHUNK // 2, :]
    last = r[CHUNK - 1 :, :]
    row, col = iota((COLS, COLS), 0), iota((COLS, COLS), 1)
    same = ((row ^ col) & (HEADS - 1)) == 0
    later = jnp.where(same & (row > col), 1.0, 0.0).astype(BF16)
    earlier = jnp.where(same & (row < col), 1.0, 0.0).astype(BF16)
    parts = [jnp.broadcast_to(part.astype(F32), (8, COLS)).astype(BF16) for part in split(last, 3)]
    after = sum(jnp.dot(part, later, preferred_element_type=F32) for part in parts)
    prior = sum(jnp.dot(part, earlier, preferred_element_type=F32) for part in parts)
    step_back = pltpu.roll(jnp.broadcast_to(last - pivot, (8, COLS)), HEADS, 1)
    alpha = jnp.where(iota((8, COLS), 1) < HEADS, 0.0, step_back) + pivot
    same = iota((HEADS, COLS), 0) == (iota((HEADS, COLS), 1) & (HEADS - 1))
    skip = exact_dot(jnp.broadcast_to(skip_ref[...], (8, HEADS)), jnp.where(same, 1.0, 0.0))
    weight = jnp.exp((last - r) + after[:1])
    w_ref[...] = weight
    store_pair(w_pair_ref, weight)
    in_ref[:CHUNK, :] = jnp.exp(pivot - r)
    in_ref[CHUNK:, :] = jnp.where(iota((8, COLS), 0) == 0, jnp.exp(alpha), skip)
    store_pair(out_ref, jnp.exp(r - pivot))
    far = jnp.exp(r + prior[:1])
    far_ref[...] = far
    store_pair(far_pair_ref, far)
    total = over_lanes(jnp.exp(after + last)[:, :128], 0, 0, WIDTH)
    hi, mid, low = (part.astype(F32) for part in split(total, 3))
    row = iota((8, WIDTH), 0)
    total_ref[...] = jnp.where(row == 0, hi, jnp.where(row == 1, mid, jnp.where(row == 2, low, 0.0))).astype(BF16)
    fill_hot(hot_ref)

    def scale_slot(i, _):
        fetch(i).wait()
        for half in range(2):
            chunk = 2 * (pos_ref[i] - base) + half
            frames = slice(half * CHUNK, (half + 1) * CHUNK)
            source, pair = w_ref[:, column_of(chunk)], w_pair_ref[:, tile_of(chunk)]
            hot = heads_of(hot_ref, chunk)
            for at in range(0, WIDTH, WIDE):
                lanes = slice(at, at + WIDE)
                if at < WIDTH // 2:
                    weight = jnp.dot(pair, hot[:, lanes], preferred_element_type=F32)
                else:
                    weight = over_lanes(source, chunk, at, WIDE)
                scaled_all[i, frames, lanes] = (x_all[i, frames, lanes].astype(F32) * weight).astype(BF16)
        put(i).start()
        return 0

    lax.fori_loop(0, SLOTS, scale_slot, 0)
    for i in range(SLOTS):
        put(i).wait()


def summary_kernel(scaled_ref, total_ref, *rest):
    pieces, (pay_ref, out_ref, proj_ref, scaled_all, acc_ref, sem, sems, piece_sems) = rest[:8], rest[8:]

    def fetch(k):
        rows = pl.ds(k * SPAN, SPAN)
        return pltpu.make_async_copy(scaled_ref.at[rows, :], scaled_all.at[rows, :], sems.at[k])

    me = lax.axis_index("head")
    loads = []
    for i, hop in enumerate((0, 2, 6, 4)):
        source = lax.rem(me + 8 - hop, 8)
        for j, shard in ((i, source), (i + 4, source ^ 1)):
            rows = pl.ds(pl.multiple_of(shard * SHARD, SHARD), SHARD)
            loads.append(pltpu.make_async_copy(pieces[j], proj_ref.at[rows, :], piece_sems.at[j]))
            loads[-1].start()
    for k in range(SPANS):
        fetch(k).start()
    for load in loads:
        load.wait()
    keep = pltpu.make_async_copy(proj_ref, out_ref, sem)
    keep.start()
    for k in range(SPANS):
        fetch(k).wait()
        rows = slice(k * SPAN, (k + 1) * SPAN)
        for at in range(0, WIDTH, WIDE):
            lanes = slice(at, at + WIDE)
            state = jnp.dot(proj_ref[:STATE, rows], scaled_all[rows, lanes], preferred_element_type=F32)
            if k > 0:
                state = acc_ref[:, lanes] + state
            if k < SPANS - 1:
                acc_ref[:, lanes] = state
                continue
            state = state.astype(BF16)
            for j in range(OWNERS):
                block, wide = block_of_slice(j)
                if at <= wide.start < at + WIDE:
                    pay_ref[j, :32, :] = state[block, wide.start - at : wide.stop - at]
                    pay_ref[j, 32:, :] = total_ref[:, wide]
    keep.wait()


def prefix_kernel(in_ref, out_ref):
    carry = jnp.zeros((32, 128), F32)
    for d in range(OWNERS):
        out_ref[d] = carry.astype(BF16)
        decay = in_ref[d, 32:, :].astype(F32)
        decay = decay[0:1] + decay[1:2] + decay[2:3]
        carry = decay * carry + in_ref[d, :32, :].astype(F32)


def near_kernel(first, slot_ref, x_ref, proj_hbm, in_hbm, scale_hbm, *rest):
    near_ref, ct_ref, last_ref, held_ref, in_ref, out_scale_ref, hot_ref, x_all, proj_all, sems = rest[-10:]
    step = pl.program_id(0)
    half_slots = SLOTS // 2

    def fetch(i):
        start = pl.multiple_of(slot_ref[i + first] * GROUP, GROUP)
        return (
            pltpu.make_async_copy(proj_hbm.at[:, pl.ds(start, GROUP)], proj_all.at[i], sems.at[half_slots + i]),
            pltpu.make_async_copy(x_ref.at[pl.ds(start, GROUP), :], x_all.at[i], sems.at[i]),
        )

    tables = [
        pltpu.make_async_copy(in_hbm, in_ref, sems.at[2 * half_slots]),
        pltpu.make_async_copy(scale_hbm, out_scale_ref, sems.at[2 * half_slots + 1]),
    ]
    if first:
        tables.append(pltpu.make_async_copy(rest[0], held_ref, sems.at[2 * half_slots + 2]))

    @pl.when(step == 0)
    def _():
        for i in range(half_slots):
            for copy in fetch(i):
                copy.start()
            if i == 0:
                for copy in tables:
                    copy.start()
        fill_hot(hot_ref)
        if not first:
            held_ref[...] = jnp.zeros_like(held_ref)
        for copy in tables:
            copy.wait()

    for copy in fetch(step):
        copy.wait()
    causal = iota((CHUNK, CHUNK), 0) >= iota((CHUNK, CHUNK), 1)
    for half in range(2):
        chunk = 2 * (step + first) + half
        frames = slice(half * CHUNK, (half + 1) * CHUNK)
        b = proj_all[step, :STATE, frames]
        c_t = proj_all[step, STATE:, frames].T
        ct_ref[frames, :] = c_t
        coupling = jnp.where(causal, jnp.dot(c_t, b, preferred_element_type=F32), 0.0).astype(BF16)
        left = jnp.concatenate([coupling, c_t], axis=1)
        to_pivot, from_pivot = in_ref[:, column_of(chunk)], out_scale_ref[:, tile_of(chunk)]
        hot = heads_of(hot_ref, chunk)
        for at in range(0, WIDTH, WIDE):
            lanes = slice(at, at + WIDE)
            scale = over_lanes(to_pivot, chunk, at, WIDE)
            x = x_all[step, frames, lanes].astype(F32)
            held = held_ref[:, lanes] * scale[CHUNK : CHUNK + 1]
            scaled = (x * scale[:CHUNK]).astype(BF16)
            held_ref[:, lanes] = held + jnp.dot(b, scaled, preferred_element_type=F32)
            right = jnp.concatenate([scaled, held.astype(BF16)], axis=0)
            mixed = jnp.dot(left, right, preferred_element_type=F32)
            back = jnp.dot(from_pivot, hot[:, lanes], preferred_element_type=F32)
            near_ref[frames, lanes] = (mixed * back + scale[CHUNK + 1 : CHUNK + 2] * x).astype(BF16)

    @pl.when(step == half_slots - 1)
    def _():
        last_ref[...] = held_ref[...]


def finish_kernel(
    near_ref, ct_hbm, far_hbm, far_pair_hbm, carry_hbm,
    out_ref, held_ref, near_all, ct_all, far_ref, far_pair_ref, carry_ref, hot_ref, sems,
):
    step = pl.program_id(0)
    steps = SLOTS // 2

    def fetch(i):
        rows = pl.ds(i * 2 * GROUP, 2 * GROUP)
        return (
            pltpu.make_async_copy(ct_hbm.at[rows, :], ct_all.at[i], sems.at[steps + i]),
            pltpu.make_async_copy(near_ref.at[rows, :], near_all.at[i], sems.at[i]),
        )

    tables = [
        pltpu.make_async_copy(source, target, sems.at[2 * steps + i])
        for i, (source, target) in enumerate(
            ((carry_hbm, carry_ref), (far_hbm, far_ref), (far_pair_hbm, far_pair_ref))
        )
    ]

    @pl.when(step == 0)
    def _():
        for copy in tables:
            copy.start()
        for i in range(steps):
            for copy in fetch(i):
                copy.start()
        fill_hot(hot_ref)
        for copy in tables:
            copy.wait()
        for j in range(OWNERS):
            held_ref[block_of_slice(j)] = carry_ref[j]

    for copy in fetch(step):
        copy.wait()
    for part in range(4):
        chunk = 4 * step + part
        frames = slice(part * CHUNK, (part + 1) * CHUNK)
        c_t = ct_all[step, frames, :]
        hot = heads_of(hot_ref, chunk)
        for at in range(0, WIDTH, WIDE):
            lanes = slice(at, at + WIDE)
            across = jnp.dot(c_t, held_ref[:, lanes], preferred_element_type=F32)
            if at < WIDE:
                far = jnp.dot(far_pair_ref[:, tile_of(chunk)], hot[:, lanes], preferred_element_type=F32)
            else:
                far = over_lanes(far_ref[:, column_of(chunk)], chunk, at, WIDE)
            near = near_all[step, frames, lanes].astype(F32)
            out_ref[frames, lanes] = (near + far * across).astype(BF16)


def shards(frames, state_proj, log_decay, skip_gain, group_pos):
    def permuted(value, steps):
        return lax.ppermute(value, "head", [(i, (i + steps) % 8) for i in range(8)])

    def partner(value):
        return lax.ppermute(value, "head", [(i, i ^ 1) for i in range(8)])

    params = pltpu.CompilerParams(vmem_limit_bytes=16 << 20)
    mid_params = pltpu.CompilerParams(vmem_limit_bytes=MID_VMEM << 20)
    wide_params = pltpu.CompilerParams(vmem_limit_bytes=WIDE_VMEM << 20)
    shape = jax.ShapeDtypeStruct
    slots, scaled, to_pivot, from_pivot, far, far_pair, total = pl.pallas_call(
        decay_kernel,
        in_specs=[
            pl.BlockSpec(memory_space=pltpu.SMEM),
            pl.BlockSpec(memory_space=pltpu.HBM),
            VMEM_SPEC,
            VMEM_SPEC,
        ],
        out_specs=[pl.BlockSpec(memory_space=pltpu.SMEM), pl.BlockSpec(memory_space=pltpu.HBM)] + [VMEM_SPEC] * 5,
        scratch_shapes=[
            pltpu.VMEM((256, WIDTH), BF16),
            pltpu.VMEM((COLS, CHUNK), F32),
            pltpu.VMEM((CHUNK, COLS), F32),
            pltpu.VMEM((CHUNK, 2 * COLS), BF16),
            pltpu.VMEM((SLOTS, GROUP, WIDTH), BF16),
            pltpu.VMEM((SLOTS, GROUP, WIDTH), BF16),
            pltpu.SemaphoreType.DMA((SLOTS,)),
            pltpu.SemaphoreType.DMA((SLOTS,)),
        ],
        out_shape=[
            shape((SLOTS,), jnp.int32),
            shape((FRAMES, WIDTH), BF16),
            shape((CHUNK + 8, COLS), F32),
            shape((CHUNK, 2 * COLS), BF16),
            shape((CHUNK, COLS), F32),
            shape((CHUNK, 2 * COLS), BF16),
            shape((EXTRA, WIDTH), BF16),
        ],
        compiler_params=pltpu.CompilerParams(vmem_limit_bytes=DECAY_VMEM << 20),
        cost_estimate=pl.CostEstimate(flops=10**9, bytes_accessed=14 * 10**6, transcendentals=10**6),
        name="decay",
    )(group_pos, frames, log_decay, skip_gain.reshape(1, HEADS))
    near = [state_proj] + [permuted(state_proj, 2 * k) for k in (1, 3, 2)]
    own_partner = partner(state_proj)
    near, total = lax.optimization_barrier((near, total))
    pieces = near + [own_partner] + [partner(piece) for piece in near[1:]]
    pay, proj = pl.pallas_call(
        summary_kernel,
        in_specs=[pl.BlockSpec(memory_space=pltpu.HBM), VMEM_SPEC] + [pl.BlockSpec(memory_space=pl.ANY)] * 8,
        out_specs=[VMEM_SPEC, pl.BlockSpec(memory_space=pltpu.HBM)],
        scratch_shapes=[
            pltpu.VMEM((2 * STATE, FRAMES), BF16),
            pltpu.VMEM((FRAMES, WIDTH), BF16),
            pltpu.VMEM((STATE, WIDTH), F32),
            pltpu.SemaphoreType.DMA,
            pltpu.SemaphoreType.DMA((SPANS,)),
            pltpu.SemaphoreType.DMA((8,)),
        ],
        out_shape=[shape((OWNERS, 32 + EXTRA, 128), BF16), shape((2 * STATE, FRAMES), BF16)],
        compiler_params=mid_params,
        name="summary",
    )(scaled, total, *pieces)
    pay = lax.all_to_all(pay, "seq", 0, 0, tiled=True)

    def near_call(first, *start_and_done):
        done = start_and_done[1:]

        return pl.pallas_call(
            functools.partial(near_kernel, first),
            grid_spec=pltpu.PrefetchScalarGridSpec(
                num_scalar_prefetch=1,
                grid=(SLOTS // 2,),
                in_specs=[pl.BlockSpec(memory_space=pltpu.HBM)] * (5 if first else 4)
                + [pl.BlockSpec(memory_space=pl.ANY)] * len(done),
                out_specs=[
                    pl.BlockSpec((GROUP, WIDTH), lambda c, *_: (c + first, 0)),
                    pl.BlockSpec((GROUP, STATE), lambda c, *_: (c + first, 0)),
                    VMEM_SPEC,
                ],
                scratch_shapes=[
                    pltpu.VMEM((STATE, WIDTH), F32),
                    pltpu.VMEM((CHUNK + 8, COLS), F32),
                    pltpu.VMEM((CHUNK, 2 * COLS), BF16),
                    pltpu.VMEM((256, WIDTH), BF16),
                    pltpu.VMEM((SLOTS // 2, GROUP, WIDTH), BF16),
                    pltpu.VMEM((SLOTS // 2, 2 * STATE, GROUP), BF16),
                    pltpu.SemaphoreType.DMA((SLOTS + 3,)),
                ],
            ),
            out_shape=[shape((FRAMES, WIDTH), BF16), shape((FRAMES, STATE), BF16), shape((STATE, WIDTH), F32)],
            input_output_aliases={6 + i: i for i in range(len(done))},
            compiler_params=wide_params,
            cost_estimate=pl.CostEstimate(flops=3 * 10**9, bytes_accessed=20 * 10**6, transcendentals=0),
            name="near",
        )(slots, frames, proj, to_pivot, from_pivot, *start_and_done)

    near, c_t, held = near_call(0)
    pay, held = lax.optimization_barrier((pay, held))
    carry = pl.pallas_call(
        prefix_kernel,
        in_specs=[VMEM_SPEC],
        out_specs=VMEM_SPEC,
        out_shape=shape((OWNERS, 32, 128), BF16),
        compiler_params=params,
        name="prefix",
    )(pay)
    carry = lax.all_to_all(carry, "seq", 0, 0, tiled=True)
    near, c_t, held = near_call(SLOTS // 2, held, near, c_t)
    return pl.pallas_call(
        finish_kernel,
        grid=(SLOTS // 2,),
        in_specs=[pl.BlockSpec(memory_space=pltpu.HBM)] * 2 + [pl.BlockSpec(memory_space=pl.ANY)] * 3,
        out_specs=pl.BlockSpec((2 * GROUP, WIDTH), lambda c: (c, 0)),
        scratch_shapes=[
            pltpu.VMEM((STATE, WIDTH), BF16),
            pltpu.VMEM((SLOTS // 2, 2 * GROUP, WIDTH), BF16),
            pltpu.VMEM((SLOTS // 2, 2 * GROUP, STATE), BF16),
            pltpu.VMEM((CHUNK, COLS), F32),
            pltpu.VMEM((CHUNK, 2 * COLS), BF16),
            pltpu.VMEM((OWNERS, 32, 128), BF16),
            pltpu.VMEM((256, WIDTH), BF16),
            pltpu.SemaphoreType.DMA((SLOTS + 3,)),
        ],
        out_shape=shape((FRAMES, WIDTH), BF16),
        compiler_params=mid_params,
        name="finish",
    )(near, c_t, far, far_pair, carry)


def solution(mesh):
    return jax.shard_map(
        shards,
        mesh=mesh,
        in_specs=(P("seq", "head"), P("head", "seq"), P("head", "seq"), P("head"), P("seq")),
        out_specs=P("seq", "head"),
        check_vma=False,
    )
```

time: 712 us -> 73.1 us (0.10)
  the two profiles are of different devices: /device:TPU:30 before, /device:TPU:4 now
where the time goes in v2:
time: 73.1 us; the launch traced here: 72.6 us
  Pallas kernels  40 us (55%)
  starting transfers between devices  21.8 us (30%)
  waiting for transfers between devices  9.31 us (13%)
  local copies, waits for them, and re-layouts  1.39 us (2%)
    pallas_call x2, Pallas kernels, near_call(): pl.pallas_call(functools.partial(near_kernel, first), grid_spec=pltpu.Pre...  19 us
    all_to_all x1, starting transfers between devices, shards(): pay = lax.all_to_all(pay, 'seq', 0, 0, tiled=True)  11.5 us
    pallas_call x1, Pallas kernels, shards(): pl.pallas_call(decay_kernel, in_specs=[pl.BlockSpec(memory_space=pltpu.SM...  7.26 us
    pallas_call x1, Pallas kernels, shards(): pl.pallas_call(finish_kernel, grid=(SLOTS // 2,), in_specs=[pl.BlockSpec(...  7.03 us
    pallas_call x1, Pallas kernels, shards(): pl.pallas_call(summary_kernel, in_specs=[pl.BlockSpec(memory_space=pltpu....  6 us
    all_to_all x1, starting transfers between devices, shards(): carry = lax.all_to_all(carry, 'seq', 0, 0, tiled=True)  5.54 us
    all_to_all x1, waiting for transfers between devices, shards(): pay = lax.all_to_all(pay, 'seq', 0, 0, tiled=True)  4.25 us
    ppermute x3, starting transfers between devices, permuted(): return lax.ppermute(value, 'head', [(i, (i + steps) % 8) for i in range(8)])  4.24 us
  transfers between devices with their start and end apart: 9, of which 7 were waited for; matrix products, arithmetic and copies ran while one was open for 0% of the time, Pallas kernels for 36%

profile of v2, /device:TPU:4, one launch (start us, length us, event | category | flops | bytes accessed | tf_op | source)
XLA Modules:
  0.0 72.6 jit_solution(16695637256825320329)
XLA Ops:
  0.0 2.2 %collective-permute-start.2 = (bf16[32,3072]{1,0:T(8,128)(2,1)}, bf16[32,3072]{1,0:T(8,128)(2,1)S(1)}, u32[]{:S(2)}, u32[]{:S(2)}) collective-permute-start(bf16[32,3072]{1,0:T(8,128)(2,1)} %rest_0_), channel_id=1, source_target_pairs={{0,4},{1,5},{2,6},{3,7},{4,0},{5,1},{6,2},{7,3},{8,12},{9,13},{10,... | collective-permute-start | bytes 589832 | tf_op jit(solution)/shard_map/ppermute | solution.py:331
  2.2 0.4 collective-permute-start.1
  2.7 1.6 %collective-permute-start = (bf16[32,3072]{1,0:T(8,128)(2,1)}, bf16[32,3072]{1,0:T(8,128)(2,1)S(1)}, u32[]{:S(2)}, u32[]{:S(2)}) collective-permute-start(bf16[32,3072]{1,0:T(8,128)(2,1)} %rest_0_), channel_id=1, source_target_pairs={{0,2},{1,3},{2,4},{3,5},{4,6},{5,7},{6,0},{7,1},{8,10},{9,11},{10,... | collective-permute-start | bytes 589832 | tf_op jit(solution)/shard_map/ppermute | solution.py:331
  4.2 0.0 collective-permute-start.3
  4.2 7.3 %decay.1 = (s32[12]{0:T(128)}, bf16[3072,1024]{1,0:T(8,128)(2,1)}, f32[136,384]{1,0:T(8,128)}, bf16[128,768]{1,0:T(8,128)(2,1)}, f32[128,384]{1,0:T(8,128)}, /*i...) custom-call(s32[12]{0:T(128)} %pos_ref.1, bf16[3072,1024]{1,0:T(8,128)(2,1)} %x_ref.5, f32[16,3072]{1,0:T(8,128)} %ld_ref.1, ...), custom_call_target="tpu_custom_call" | custom-call | flops 1000000000 | bytes 14000000 | tf_op jit(solution)/shard_map/decay/pallas_call | solution.py:340
  11.5 0.0 collective-permute-done.2.rest_3_
  11.5 0.0 copy-start.1
  11.5 0.2 collective-permute-done.1.rest_2_
  11.7 0.9 %collective-permute-done.rest_1_ = bf16[32,3072]{1,0:T(8,128)(2,1)S(1)} collective-permute-done((bf16[32,3072]{1,0:T(8,128)(2,1)}, bf16[32,3072]{1,0:T(8,128)(2,1)S(1)}, u32[]{:S(2)}, u32[]{:S(2)}) %collective-permute-start) | collective-permute-done | bytes 196640 | tf_op jit(solution)/shard_map/ppermute | solution.py:331
  12.6 0.0 collective-permute-start.4
  12.6 0.5 collective-permute-start.5
  13.1 0.0 collective-permute-start.6
  13.1 0.0 collective-permute-done.3.rest_4_
  13.1 0.9 %collective-permute-done.4.rest_5_ = bf16[32,3072]{1,0:T(8,128)(2,1)S(1)} collective-permute-done((bf16[32,3072]{1,0:T(8,128)(2,1)S(1)}, bf16[32,3072]{1,0:T(8,128)(2,1)S(1)}, u32[]{:S(2)}, u32[]{:S(2)}) %collective-permute-start.4) | collective-permute-done | bytes 196640 | tf_op jit(solution)/shard_map/ppermute | solution.py:334
  14.0 0.3 collective-permute-done.5.rest_6_
  14.3 0.3 collective-permute-done.6.rest_7_
  14.6 0.0 copy-done.1
  14.6 0.0 copy-done.2
  14.6 0.0 copy-done.3
  14.6 0.1 copy-done.5
  14.7 0.3 copy-done.6
  15.0 0.3 copy-done.7
  15.3 6.0 %summary.1 = (bf16[32,40,128]{2,1,0:T(8,128)(2,1)}, bf16[256,3072]{1,0:T(8,128)(2,1)}) custom-call(bf16[3072,1024]{1,0:T(8,128)(2,1)} %get-tuple-element.27.scaled_ref, bf16[8,1024]{1,0:T(8,128)(2,1)} %get-tuple-element.29.total_ref, bf16[32,3072]{1,0:T(8,128)(2,1)} %rest_0_, bf16[32,3072]{1,0:T(8,128)(2,1)} %copy-done.3, bf16[32,3072]{1,0:T(8,128)(2,1)} %copy-done.2, ...), custom_call_target="tpu_custom_call" | custom-call | tf_op jit(solution)/shard_map/summary/pallas_call | solution.py:376
  21.3 11.5 %all-to-all-start = ((bf16[32,40,128]{2,1,0:T(8,128)(2,1)}), bf16[32,40,128]{2,1,0:T(8,128)(2,1)S(1)}, u32[]{:S(2)}, u32[]{:S(2)}) async-start(bf16[32,40,128]{2,1,0:T(8,128)(2,1)} %get-tuple-element.37), calls=%async_computation | async-start | bytes 655360 | tf_op jit(solution)/shard_map/all_to_all | solution.py:392
  32.8 9.3 %near.2 = (bf16[3072,1024]{1,0:T(8,128)(2,1)}, bf16[3072,128]{1,0:T(8,128)(2,1)}, f32[128,1024]{1,0:T(8,128)}) custom-call(s32[12]{0:T(128)} %get-tuple-element.26.slot_ref, bf16[3072,1024]{1,0:T(8,128)(2,1)} %x_ref.5, bf16[256,3072]{1,0:T(8,128)(2,1)} %get-tuple-element.34.proj_hbm, f32[136,384]{1,0:T(8,128)} %get-tuple-element.35.in_hbm, ...), custom_call_target="tpu_custom_call" | custom-call | flops 3000000000 | bytes 20000000 | tf_op jit(solution)/shard_map/near/pallas_call | solution.py:397
  42.1 4.2 %all-to-all-done.in_ref = bf16[32,40,128]{2,1,0:T(8,128)(2,1)S(1)} async-done(((bf16[32,40,128]{2,1,0:T(8,128)(2,1)}), bf16[32,40,128]{2,1,0:T(8,128)(2,1)S(1)}, u32[]{:S(2)}, u32[]{:S(2)}) %all-to-all-start) | async-done | bytes 327712 | tf_op jit(solution)/shard_map/all_to_all | solution.py:392
  46.4 0.8 %prefix.1 = bf16[32,32,128]{2,1,0:T(8,128)(2,1)} custom-call(bf16[32,40,128]{2,1,0:T(8,128)(2,1)S(1)} %all-to-all-done.in_ref), custom_call_target="tpu_custom_call" | custom-call | tf_op jit(solution)/shard_map/prefix/pallas_call | solution.py:428
  47.1 5.5 %all-to-all-start.1 = ((bf16[32,32,128]{2,1,0:T(8,128)(2,1)}), bf16[32,32,128]{2,1,0:T(8,128)(2,1)S(1)}, u32[]{:S(2)}, u32[]{:S(2)}) async-start(bf16[32,32,128]{2,1,0:T(8,128)(2,1)} %prefix.1), calls=%async_computation.1 | async-start | bytes 524288 | tf_op jit(solution)/shard_map/all_to_all | solution.py:436
  52.7 9.6 %near.3 = (bf16[3072,1024]{1,0:T(8,128)(2,1)}, bf16[3072,128]{1,0:T(8,128)(2,1)}, f32[128,1024]{1,0:T(8,128)}) custom-call(s32[12]{0:T(128)} %get-tuple-element.26.slot_ref, bf16[3072,1024]{1,0:T(8,128)(2,1)} %x_ref.5, bf16[256,3072]{1,0:T(8,128)(2,1)} %get-tuple-element.34.proj_hbm, ...), custom_call_target="tpu_custom_call", output_to_operand_aliasing={{0}: (6, {}), {1}: (7, {})} | custom-call | flops 3000000000 | bytes 20000000 | tf_op jit(solution)/shard_map/near/pallas_call | solution.py:397
  62.3 2.6 %all-to-all-done.1.carry_hbm = bf16[32,32,128]{2,1,0:T(8,128)(2,1)S(1)} async-done(((bf16[32,32,128]{2,1,0:T(8,128)(2,1)}), bf16[32,32,128]{2,1,0:T(8,128)(2,1)S(1)}, u32[]{:S(2)}, u32[]{:S(2)}) %all-to-all-start.1) | async-done | bytes 262176 | tf_op jit(solution)/shard_map/all_to_all | solution.py:436
  64.9 0.7 copy-done
  65.6 7.0 %finish.1 = bf16[3072,1024]{1,0:T(8,128)(2,1)} custom-call(bf16[3072,1024]{1,0:T(8,128)(2,1)} %get-tuple-element.42.near_ref, bf16[3072,128]{1,0:T(8,128)(2,1)} %get-tuple-element.43.ct_hbm, f32[128,384]{1,0:T(8,128)} %get-tuple-element.44.far_hbm, bf16[128,768]{1,0:T(8,128)(2,1)} %get-tuple-element.45.far_pair_hbm, bf16[32,32,128]{2,1,0:T(8,128)(2,1)} %copy-done), custom_call_target="tpu_custom_call" | custom-call | tf_op jit(solution)/shard_map/finish/pallas_call | solution.py:438
  (8 shorter events, 0.0 us)
Async XLA Ops:
  0.0 11.5 %collective-permute-start.2 = (bf16[32,3072]{1,0:T(8,128)(2,1)}, bf16[32,3072]{1,0:T(8,128)(2,1)S(1)}, u32[]{:S(2)}, u32[]{:S(2)}) collective-permute-start(bf16[32,3072]{1,0:T(8,128)(2,1)} %rest_0_), channel_id=1, source_target_pairs={{0,4},{1,5},{2,6},{3,7},{4,0},{5,1},{6,2},{7,3},{8,12},{9,13},{10,... | collective-permute-start | bytes 589832 | tf_op jit(solution)/shard_map/ppermute | solution.py:331
  2.2 9.5 %collective-permute-start.1 = (bf16[32,3072]{1,0:T(8,128)(2,1)}, bf16[32,3072]{1,0:T(8,128)(2,1)S(1)}, u32[]{:S(2)}, u32[]{:S(2)}) collective-permute-start(bf16[32,3072]{1,0:T(8,128)(2,1)} %rest_0_), channel_id=1, source_target_pairs={{0,6},{1,7},{2,0},{3,1},{4,2},{5,3},{6,4},{7,5},{8,14},{9,15},{10,... | collective-permute-start | bytes 589832 | tf_op jit(solution)/shard_map/ppermute | solution.py:331
  2.7 9.9 %collective-permute-start = (bf16[32,3072]{1,0:T(8,128)(2,1)}, bf16[32,3072]{1,0:T(8,128)(2,1)S(1)}, u32[]{:S(2)}, u32[]{:S(2)}) collective-permute-start(bf16[32,3072]{1,0:T(8,128)(2,1)} %rest_0_), channel_id=1, source_target_pairs={{0,2},{1,3},{2,4},{3,5},{4,6},{5,7},{6,0},{7,1},{8,10},{9,11},{10,... | collective-permute-start | bytes 589832 | tf_op jit(solution)/shard_map/ppermute | solution.py:331
  4.2 8.9 %collective-permute-start.3 = (bf16[32,3072]{1,0:T(8,128)(2,1)}, bf16[32,3072]{1,0:T(8,128)(2,1)S(1)}, u32[]{:S(2)}, u32[]{:S(2)}) collective-permute-start(bf16[32,3072]{1,0:T(8,128)(2,1)} %rest_0_), channel_id=1, source_target_pairs={{0,1},{1,0},{2,3},{3,2},{4,5},{5,4},{6,7},{7,6},{8,9},{9,8},{10,11... | collective-permute-start | bytes 589832 | tf_op jit(solution)/shard_map/ppermute | solution.py:334
  11.5 3.1 %copy-start.1 = (bf16[32,3072]{1,0:T(8,128)(2,1)}, bf16[32,3072]{1,0:T(8,128)(2,1)S(1)}, u32[]{:S(2)}) copy-start(bf16[32,3072]{1,0:T(8,128)(2,1)S(1)} %collective-permute-done.2.rest_3_) | copy-start | bytes 589828
  11.7 2.9 %copy-start.2 = (bf16[32,3072]{1,0:T(8,128)(2,1)}, bf16[32,3072]{1,0:T(8,128)(2,1)S(1)}, u32[]{:S(2)}) copy-start(bf16[32,3072]{1,0:T(8,128)(2,1)S(1)} %collective-permute-done.1.rest_2_) | copy-start | bytes 589828
  12.6 2.0 %copy-start.3 = (bf16[32,3072]{1,0:T(8,128)(2,1)}, bf16[32,3072]{1,0:T(8,128)(2,1)S(1)}, u32[]{:S(2)}) copy-start(bf16[32,3072]{1,0:T(8,128)(2,1)S(1)} %collective-permute-done.rest_1_) | copy-start | bytes 589828
  12.6 1.4 %collective-permute-start.4 = (bf16[32,3072]{1,0:T(8,128)(2,1)S(1)}, bf16[32,3072]{1,0:T(8,128)(2,1)S(1)}, u32[]{:S(2)}, u32[]{:S(2)}) collective-permute-start(bf16[32,3072]{1,0:T(8,128)(2,1)S(1)} %collective-permute-done.rest_1_), channel_id=1, source_target_pairs={{0,1},{1,0},{2,3},{3,2},{4,5},{5,4},{6,7},{7,6},{8,9},{9,8},{10,11... | collective-permute-start | bytes 589832 | tf_op jit(solution)/shard_map/ppermute | solution.py:334
  12.6 1.7 %collective-permute-start.5 = (bf16[32,3072]{1,0:T(8,128)(2,1)S(1)}, bf16[32,3072]{1,0:T(8,128)(2,1)S(1)}, u32[]{:S(2)}, u32[]{:S(2)}) collective-permute-start(bf16[32,3072]{1,0:T(8,128)(2,1)S(1)} %collective-permute-done.1.rest_2_), channel_id=1, source_target_pairs={{0,1},{1,0},{2,3},{3,2},{4,5},{5,4},{6,7},{7,6},{8,9},{9,8},{10,11... | collective-permute-start | bytes 589832 | tf_op jit(solution)/shard_map/ppermute | solution.py:334
  13.1 1.5 %collective-permute-start.6 = (bf16[32,3072]{1,0:T(8,128)(2,1)S(1)}, bf16[32,3072]{1,0:T(8,128)(2,1)S(1)}, u32[]{:S(2)}, u32[]{:S(2)}) collective-permute-start(bf16[32,3072]{1,0:T(8,128)(2,1)S(1)} %collective-permute-done.2.rest_3_), channel_id=1, source_target_pairs={{0,1},{1,0},{2,3},{3,2},{4,5},{5,4},{6,7},{7,6},{8,9},{9,8},{10,11... | collective-permute-start | bytes 589832 | tf_op jit(solution)/shard_map/ppermute | solution.py:334
  13.1 1.5 %copy-start.4 = (bf16[32,3072]{1,0:T(8,128)(2,1)}, bf16[32,3072]{1,0:T(8,128)(2,1)S(1)}, u32[]{:S(2)}) copy-start(bf16[32,3072]{1,0:T(8,128)(2,1)S(1)} %collective-permute-done.3.rest_4_) | copy-start | bytes 589828
  14.0 0.7 copy-start.5
  14.3 0.7 copy-start.6
  14.6 0.7 copy-start.7
  21.3 25.1 %all-to-all-start = ((bf16[32,40,128]{2,1,0:T(8,128)(2,1)}), bf16[32,40,128]{2,1,0:T(8,128)(2,1)S(1)}, u32[]{:S(2)}, u32[]{:S(2)}) async-start(bf16[32,40,128]{2,1,0:T(8,128)(2,1)} %get-tuple-element.37), calls=%async_computation | async-start | bytes 655360 | tf_op jit(solution)/shard_map/all_to_all | solution.py:392
  47.1 17.8 %all-to-all-start.1 = ((bf16[32,32,128]{2,1,0:T(8,128)(2,1)}), bf16[32,32,128]{2,1,0:T(8,128)(2,1)S(1)}, u32[]{:S(2)}, u32[]{:S(2)}) async-start(bf16[32,32,128]{2,1,0:T(8,128)(2,1)} %prefix.1), calls=%async_computation.1 | async-start | bytes 524288 | tf_op jit(solution)/shard_map/all_to_all | solution.py:436
  64.9 0.7 copy-start

commit v3 on v2

--- a/solution.py
+++ b/solution.py
@@ -20,12 +20,11 @@
 SHARD = 32
 OWNERS = 32
 EXTRA = 8
-DECAY_VMEM = 58
+DECAY_VMEM = 44
+SUMMARY_VMEM = 16
 WIDE_VMEM = 58
-MID_VMEM = 58
+MID_VMEM = 53
 WIDE = 256
-SPANS = 4
-SPAN = FRAMES // SPANS
 F32, BF16 = jnp.float32, jnp.bfloat16
 VMEM_SPEC = pl.BlockSpec(memory_space=pltpu.VMEM)
 
@@ -88,13 +87,10 @@
 def decay_kernel(
     pos_ref, x_ref, ld_ref, skip_ref,
     slot_ref, scaled_ref, in_ref, out_ref, far_ref, far_pair_ref, total_ref,
-    hot_ref, log_ref, w_ref, w_pair_ref, x_all, scaled_all, sems, out_sems,
+    hot_ref, log_ref, w_ref, w_pair_ref, x_all, sems,
 ):
     def fetch(i):
         return pltpu.make_async_copy(x_ref.at[pl.ds(i * GROUP, GROUP), :], x_all.at[i], sems.at[i])
-
-    def put(i):
-        return pltpu.make_async_copy(scaled_all.at[i], scaled_ref.at[pl.ds(i * GROUP, GROUP), :], out_sems.at[i])
 
     for i in range(SLOTS):
         fetch(i).start()
@@ -152,53 +148,28 @@
                     weight = jnp.dot(pair, hot[:, lanes], preferred_element_type=F32)
                 else:
                     weight = over_lanes(source, chunk, at, WIDE)
-                scaled_all[i, frames, lanes] = (x_all[i, frames, lanes].astype(F32) * weight).astype(BF16)
-        put(i).start()
+                scaled_ref[pl.ds(pl.multiple_of(i * GROUP + half * CHUNK, CHUNK), CHUNK), lanes] = (x_all[i, frames, lanes].astype(F32) * weight).astype(BF16)
         return 0
 
     lax.fori_loop(0, SLOTS, scale_slot, 0)
-    for i in range(SLOTS):
-        put(i).wait()
 
 
 def summary_kernel(scaled_ref, total_ref, *rest):
-    pieces, (pay_ref, out_ref, proj_ref, scaled_all, acc_ref, sem, sems, piece_sems) = rest[:8], rest[8:]
-
-    def fetch(k):
-        rows = pl.ds(k * SPAN, SPAN)
-        return pltpu.make_async_copy(scaled_ref.at[rows, :], scaled_all.at[rows, :], sems.at[k])
-
+    pieces, (pay_ref, out_ref, proj_ref, sem) = rest[:8], rest[8:]
     me = lax.axis_index("head")
-    loads = []
     for i, hop in enumerate((0, 2, 6, 4)):
         source = lax.rem(me + 8 - hop, 8)
-        for j, shard in ((i, source), (i + 4, source ^ 1)):
-            rows = pl.ds(pl.multiple_of(shard * SHARD, SHARD), SHARD)
-            loads.append(pltpu.make_async_copy(pieces[j], proj_ref.at[rows, :], piece_sems.at[j]))
-            loads[-1].start()
-    for k in range(SPANS):
-        fetch(k).start()
-    for load in loads:
-        load.wait()
+        proj_ref[pl.ds(pl.multiple_of(source * SHARD, SHARD), SHARD), :] = pieces[i][...]
+        proj_ref[pl.ds(pl.multiple_of((source ^ 1) * SHARD, SHARD), SHARD), :] = pieces[i + 4][...]
     keep = pltpu.make_async_copy(proj_ref, out_ref, sem)
     keep.start()
-    for k in range(SPANS):
-        fetch(k).wait()
-        rows = slice(k * SPAN, (k + 1) * SPAN)
-        for at in range(0, WIDTH, WIDE):
-            lanes = slice(at, at + WIDE)
-            state = jnp.dot(proj_ref[:STATE, rows], scaled_all[rows, lanes], preferred_element_type=F32)
-            if k > 0:
-                state = acc_ref[:, lanes] + state
-            if k < SPANS - 1:
-                acc_ref[:, lanes] = state
-                continue
-            state = state.astype(BF16)
-            for j in range(OWNERS):
-                block, wide = block_of_slice(j)
-                if at <= wide.start < at + WIDE:
-                    pay_ref[j, :32, :] = state[block, wide.start - at : wide.stop - at]
-                    pay_ref[j, 32:, :] = total_ref[:, wide]
+    for at in range(0, WIDTH, WIDE):
+        state = jnp.dot(proj_ref[:STATE, :], scaled_ref[:, at : at + WIDE], preferred_element_type=F32).astype(BF16)
+        for j in range(OWNERS):
+            rows, lanes = block_of_slice(j)
+            if at <= lanes.start < at + WIDE:
+                pay_ref[j, :32, :] = state[rows, lanes.start - at : lanes.stop - at]
+                pay_ref[j, 32:, :] = total_ref[:, lanes]
     keep.wait()
 
 
@@ -345,15 +316,13 @@
             VMEM_SPEC,
             VMEM_SPEC,
         ],
-        out_specs=[pl.BlockSpec(memory_space=pltpu.SMEM), pl.BlockSpec(memory_space=pltpu.HBM)] + [VMEM_SPEC] * 5,
+        out_specs=[pl.BlockSpec(memory_space=pltpu.SMEM)] + [VMEM_SPEC] * 6,
         scratch_shapes=[
             pltpu.VMEM((256, WIDTH), BF16),
             pltpu.VMEM((COLS, CHUNK), F32),
             pltpu.VMEM((CHUNK, COLS), F32),
             pltpu.VMEM((CHUNK, 2 * COLS), BF16),
             pltpu.VMEM((SLOTS, GROUP, WIDTH), BF16),
-            pltpu.VMEM((SLOTS, GROUP, WIDTH), BF16),
-            pltpu.SemaphoreType.DMA((SLOTS,)),
             pltpu.SemaphoreType.DMA((SLOTS,)),
         ],
         out_shape=[
@@ -375,18 +344,14 @@
     pieces = near + [own_partner] + [partner(piece) for piece in near[1:]]
     pay, proj = pl.pallas_call(
         summary_kernel,
-        in_specs=[pl.BlockSpec(memory_space=pltpu.HBM), VMEM_SPEC] + [pl.BlockSpec(memory_space=pl.ANY)] * 8,
+        in_specs=[VMEM_SPEC] * 10,
         out_specs=[VMEM_SPEC, pl.BlockSpec(memory_space=pltpu.HBM)],
         scratch_shapes=[
             pltpu.VMEM((2 * STATE, FRAMES), BF16),
-            pltpu.VMEM((FRAMES, WIDTH), BF16),
-            pltpu.VMEM((STATE, WIDTH), F32),
             pltpu.SemaphoreType.DMA,
-            pltpu.SemaphoreType.DMA((SPANS,)),
-            pltpu.SemaphoreType.DMA((8,)),
         ],
         out_shape=[shape((OWNERS, 32 + EXTRA, 128), BF16), shape((2 * STATE, FRAMES), BF16)],
-        compiler_params=mid_params,
+        compiler_params=pltpu.CompilerParams(vmem_limit_bytes=SUMMARY_VMEM << 20),
         name="summary",
     )(scaled, total, *pieces)
     pay = lax.all_to_all(pay, "seq", 0, 0, tiled=True)

time: 73.1 us -> 69.4 us (0.949)
  Pallas kernels: 40 us -> 34.5 us
  local copies, waits for them, and re-layouts: 1.39 us -> 3.39 us
    pallas_call x1, Pallas kernels: 6 us -> 1.99 us  [shards(): pl.pallas_call(summary_kernel, in_specs=[VMEM_SPEC] * 10, out_specs=[VMEM...]
    unnamed x16, local copies, waits for them, and re-layouts: 1.39 us -> 3.39 us
    pallas_call x1, Pallas kernels: 7.26 us -> 5.4 us  [shards(): pl.pallas_call(decay_kernel, in_specs=[pl.BlockSpec(memory_space=pltpu.SM...]
  transfers between devices with their start and end apart: 9 -> 9, of which waited for: 7 -> 6; matrix products, arithmetic and copies ran while one was open for 0% -> 0% of each run, Pallas kernels for 36% -> 35%
where the time goes in v3:
time: 69.4 us; the launch traced here: 68.7 us
  Pallas kernels  34.5 us (50%)
  starting transfers between devices  21.8 us (31%)
  waiting for transfers between devices  8.91 us (13%)
  local copies, waits for them, and re-layouts  3.39 us (5%)
    pallas_call x2, Pallas kernels, near_call(): pl.pallas_call(functools.partial(near_kernel, first), grid_spec=pltpu.Pre...  19 us
    all_to_all x1, starting transfers between devices, shards(): pay = lax.all_to_all(pay, 'seq', 0, 0, tiled=True)  11.5 us
    pallas_call x1, Pallas kernels, shards(): pl.pallas_call(finish_kernel, grid=(SLOTS // 2,), in_specs=[pl.BlockSpec(...  7.3 us
    all_to_all x1, starting transfers between devices, shards(): carry = lax.all_to_all(carry, 'seq', 0, 0, tiled=True)  5.54 us
    pallas_call x1, Pallas kernels, shards(): pl.pallas_call(decay_kernel, in_specs=[pl.BlockSpec(memory_space=pltpu.SM...  5.4 us
    all_to_all x1, waiting for transfers between devices, shards(): pay = lax.all_to_all(pay, 'seq', 0, 0, tiled=True)  4.25 us
    ppermute x3, starting transfers between devices, permuted(): return lax.ppermute(value, 'head', [(i, (i + steps) % 8) for i in range(8)])  4.24 us
    unnamed x16, local copies, waits for them, and re-layouts  3.39 us
  transfers between devices with their start and end apart: 9, of which 6 were waited for; matrix products, arithmetic and copies ran while one was open for 0% of the time, Pallas kernels for 35%

profile of v3, /device:TPU:4, one launch (start us, length us, event | category | flops | bytes accessed | tf_op | source)
XLA Modules:
  0.0 68.7 jit_solution(6476477421917215689)
XLA Ops:
  0.0 2.2 %collective-permute-start.2 = (bf16[32,3072]{1,0:T(8,128)(2,1)}, bf16[32,3072]{1,0:T(8,128)(2,1)S(1)}, u32[]{:S(2)}, u32[]{:S(2)}) collective-permute-start(bf16[32,3072]{1,0:T(8,128)(2,1)} %rest_0_), channel_id=1, source_target_pairs={{0,4},{1,5},{2,6},{3,7},{4,0},{5,1},{6,2},{7,3},{8,12},{9,13},{10,... | collective-permute-start | bytes 589832 | tf_op jit(solution)/shard_map/ppermute | solution.py:302
  2.2 0.4 collective-permute-start.1
  2.7 1.6 %collective-permute-start = (bf16[32,3072]{1,0:T(8,128)(2,1)}, bf16[32,3072]{1,0:T(8,128)(2,1)S(1)}, u32[]{:S(2)}, u32[]{:S(2)}) collective-permute-start(bf16[32,3072]{1,0:T(8,128)(2,1)} %rest_0_), channel_id=1, source_target_pairs={{0,2},{1,3},{2,4},{3,5},{4,6},{5,7},{6,0},{7,1},{8,10},{9,11},{10,... | collective-permute-start | bytes 589832 | tf_op jit(solution)/shard_map/ppermute | solution.py:302
  4.2 0.0 collective-permute-start.3
  4.2 0.9 %copy-done.3 = f32[16,3072]{1,0:T(8,128)S(1)} copy-done((f32[16,3072]{1,0:T(8,128)S(1)}, f32[16,3072]{1,0:T(8,128)}, u32[]{:S(2)}) %copy-start.3) | copy-done | bytes 196632
  5.2 0.7 copy-done.6
  5.8 0.7 copy-done.7
  6.5 5.4 %decay.1 = (s32[12]{0:T(128)S(1)}, bf16[3072,1024]{1,0:T(8,128)(2,1)S(1)}, f32[136,384]{1,0:T(8,128)S(1)}, bf16[128,768]{1,0:T(8,128)(2,1)S(1)}, f32[128,384]{1,...) custom-call(s32[12]{0:T(128)S(1)} %copy-done.6, bf16[3072,1024]{1,0:T(8,128)(2,1)} %x_ref.5, ...), custom_call_target="tpu_custom_call" | custom-call | flops 1000000000 | bytes 14000000 | tf_op jit(solution)/shard_map/decay/pallas_call | solution.py:311
  11.9 0.0 collective-permute-done.2.rest_3_
  11.9 0.0 collective-permute-done.1.rest_2_
  11.9 0.6 collective-permute-done.rest_1_
  12.6 0.0 collective-permute-start.4
  12.6 0.5 collective-permute-start.5
  13.1 0.0 collective-permute-start.6
  13.1 0.0 collective-permute-done.3.rest_4_
  13.1 0.9 %collective-permute-done.4.rest_5_ = bf16[32,3072]{1,0:T(8,128)(2,1)S(1)} collective-permute-done((bf16[32,3072]{1,0:T(8,128)(2,1)S(1)}, bf16[32,3072]{1,0:T(8,128)(2,1)S(1)}, u32[]{:S(2)}, u32[]{:S(2)}) %collective-permute-start.4) | collective-permute-done | bytes 196640 | tf_op jit(solution)/shard_map/ppermute | solution.py:305
  14.0 0.3 collective-permute-done.5.rest_6_
  14.3 0.3 collective-permute-done.6.rest_7_
  14.6 2.0 %summary.1 = (bf16[32,40,128]{2,1,0:T(8,128)(2,1)}, bf16[256,3072]{1,0:T(8,128)(2,1)S(1)}) custom-call(bf16[3072,1024]{1,0:T(8,128)(2,1)S(1)} %get-tuple-element.27.scaled_ref, bf16[8,1024]{1,0:T(8,128)(2,1)S(1)} %get-tuple-element.29.total_ref, bf16[32,3072]{1,0:T(8,128)(2,1)S(1)} %copy-done.4, bf16[32,3072]{1,0:T(8,128)(2,1)S(1)} %collective-permute-done.rest_1_, ...), custom_call_target="tpu_custom_call" | custom-call | tf_op jit(solution)/shard_map/summary/pallas_call | solution.py:345
  16.6 0.0 copy-done.1
  16.6 0.0 copy-done.2
  16.6 0.0 copy-done.5
  16.6 0.0 copy-start
  16.6 1.1 %copy-done = bf16[256,3072]{1,0:T(8,128)(2,1)} copy-done((bf16[256,3072]{1,0:T(8,128)(2,1)}, bf16[256,3072]{1,0:T(8,128)(2,1)S(1)}, u32[]{:S(2)}) %copy-start) | copy-done | bytes 1572888
  17.8 11.5 %all-to-all-start = ((bf16[32,40,128]{2,1,0:T(8,128)(2,1)}), bf16[32,40,128]{2,1,0:T(8,128)(2,1)S(1)}, u32[]{:S(2)}, u32[]{:S(2)}) async-start(bf16[32,40,128]{2,1,0:T(8,128)(2,1)} %get-tuple-element.37), calls=%async_computation | async-start | bytes 655360 | tf_op jit(solution)/shard_map/all_to_all | solution.py:357
  29.2 9.3 %near.2 = (bf16[3072,1024]{1,0:T(8,128)(2,1)}, bf16[3072,128]{1,0:T(8,128)(2,1)}, f32[128,1024]{1,0:T(8,128)}) custom-call(s32[12]{0:T(128)} %copy-done.5, bf16[3072,1024]{1,0:T(8,128)(2,1)} %x_ref.5, bf16[256,3072]{1,0:T(8,128)(2,1)} %copy-done, f32[136,384]{1,0:T(8,128)} %copy-done.1, bf16[128,768]{1,0:T(8,128)(2,1)} %copy-done.2), custom_call_target="tpu_custom_call" | custom-call | flops 3000000000 | bytes 20000000 | tf_op jit(solution)/shard_map/near/pallas_call | solution.py:362
  38.6 4.3 %all-to-all-done.in_ref = bf16[32,40,128]{2,1,0:T(8,128)(2,1)S(1)} async-done(((bf16[32,40,128]{2,1,0:T(8,128)(2,1)}), bf16[32,40,128]{2,1,0:T(8,128)(2,1)S(1)}, u32[]{:S(2)}, u32[]{:S(2)}) %all-to-all-start) | async-done | bytes 327712 | tf_op jit(solution)/shard_map/all_to_all | solution.py:357
  42.8 0.8 %prefix.1 = bf16[32,32,128]{2,1,0:T(8,128)(2,1)} custom-call(bf16[32,40,128]{2,1,0:T(8,128)(2,1)S(1)} %all-to-all-done.in_ref), custom_call_target="tpu_custom_call" | custom-call | tf_op jit(solution)/shard_map/prefix/pallas_call | solution.py:393
  43.7 5.5 %all-to-all-start.1 = ((bf16[32,32,128]{2,1,0:T(8,128)(2,1)}), bf16[32,32,128]{2,1,0:T(8,128)(2,1)S(1)}, u32[]{:S(2)}, u32[]{:S(2)}) async-start(bf16[32,32,128]{2,1,0:T(8,128)(2,1)} %prefix.1), calls=%async_computation.1 | async-start | bytes 524288 | tf_op jit(solution)/shard_map/all_to_all | solution.py:401
  49.2 9.6 %near.3 = (bf16[3072,1024]{1,0:T(8,128)(2,1)}, bf16[3072,128]{1,0:T(8,128)(2,1)}, f32[128,1024]{1,0:T(8,128)}) custom-call(s32[12]{0:T(128)} %copy-done.5, bf16[3072,1024]{1,0:T(8,128)(2,1)} %x_ref.5, bf16[256,3072]{1,0:T(8,128)(2,1)} %copy-done, f32[136,384]{1,0:T(8,128)} %copy-done.1, ...), custom_call_target="tpu_custom_call", output_to_operand_aliasing={{0}: (6, {}), {1}: (7, {})} | custom-call | flops 3000000000 | bytes 20000000 | tf_op jit(solution)/shard_map/near/pallas_call | solution.py:362
  58.9 2.5 %all-to-all-done.1.carry_hbm = bf16[32,32,128]{2,1,0:T(8,128)(2,1)S(1)} async-done(((bf16[32,32,128]{2,1,0:T(8,128)(2,1)}), bf16[32,32,128]{2,1,0:T(8,128)(2,1)S(1)}, u32[]{:S(2)}, u32[]{:S(2)}) %all-to-all-start.1) | async-done | bytes 262176 | tf_op jit(solution)/shard_map/all_to_all | solution.py:401
  61.4 7.3 %finish.1 = bf16[3072,1024]{1,0:T(8,128)(2,1)} custom-call(bf16[3072,1024]{1,0:T(8,128)(2,1)} %get-tuple-element.42.near_ref, bf16[3072,128]{1,0:T(8,128)(2,1)} %get-tuple-element.43.ct_hbm, f32[128,384]{1,0:T(8,128)S(1)} %get-tuple-element.44.far_hbm, bf16[128,768]{1,0:T(8,128)(2,1)S(1)} %get-tuple-element.45.far_pair_hbm, ...), custom_call_target="tpu_custom_call" | custom-call | tf_op jit(solution)/shard_map/finish/pallas_call | solution.py:403
  (8 shorter events, 0.0 us)
Async XLA Ops:
  0.0 11.9 %collective-permute-start.2 = (bf16[32,3072]{1,0:T(8,128)(2,1)}, bf16[32,3072]{1,0:T(8,128)(2,1)S(1)}, u32[]{:S(2)}, u32[]{:S(2)}) collective-permute-start(bf16[32,3072]{1,0:T(8,128)(2,1)} %rest_0_), channel_id=1, source_target_pairs={{0,4},{1,5},{2,6},{3,7},{4,0},{5,1},{6,2},{7,3},{8,12},{9,13},{10,... | collective-permute-start | bytes 589832 | tf_op jit(solution)/shard_map/ppermute | solution.py:302
  2.2 9.7 %collective-permute-start.1 = (bf16[32,3072]{1,0:T(8,128)(2,1)}, bf16[32,3072]{1,0:T(8,128)(2,1)S(1)}, u32[]{:S(2)}, u32[]{:S(2)}) collective-permute-start(bf16[32,3072]{1,0:T(8,128)(2,1)} %rest_0_), channel_id=1, source_target_pairs={{0,6},{1,7},{2,0},{3,1},{4,2},{5,3},{6,4},{7,5},{8,14},{9,15},{10,... | collective-permute-start | bytes 589832 | tf_op jit(solution)/shard_map/ppermute | solution.py:302
  2.7 9.9 %collective-permute-start = (bf16[32,3072]{1,0:T(8,128)(2,1)}, bf16[32,3072]{1,0:T(8,128)(2,1)S(1)}, u32[]{:S(2)}, u32[]{:S(2)}) collective-permute-start(bf16[32,3072]{1,0:T(8,128)(2,1)} %rest_0_), channel_id=1, source_target_pairs={{0,2},{1,3},{2,4},{3,5},{4,6},{5,7},{6,0},{7,1},{8,10},{9,11},{10,... | collective-permute-start | bytes 589832 | tf_op jit(solution)/shard_map/ppermute | solution.py:302
  4.2 8.9 %collective-permute-start.3 = (bf16[32,3072]{1,0:T(8,128)(2,1)}, bf16[32,3072]{1,0:T(8,128)(2,1)S(1)}, u32[]{:S(2)}, u32[]{:S(2)}) collective-permute-start(bf16[32,3072]{1,0:T(8,128)(2,1)} %rest_0_), channel_id=1, source_target_pairs={{0,1},{1,0},{2,3},{3,2},{4,5},{5,4},{6,7},{7,6},{8,9},{9,8},{10,11... | collective-permute-start | bytes 589832 | tf_op jit(solution)/shard_map/ppermute | solution.py:305
  4.2 0.9 %copy-start.3 = (f32[16,3072]{1,0:T(8,128)S(1)}, f32[16,3072]{1,0:T(8,128)}, u32[]{:S(2)}) copy-start(f32[16,3072]{1,0:T(8,128)} %ld_ref.1) | copy-start | bytes 589828
  5.2 0.7 copy-start.6
  5.8 0.7 copy-start.7
  6.5 8.1 %copy-start.4 = (bf16[32,3072]{1,0:T(8,128)(2,1)S(1)}, bf16[32,3072]{1,0:T(8,128)(2,1)}, u32[]{:S(2)}) copy-start(bf16[32,3072]{1,0:T(8,128)(2,1)} %rest_0_) | copy-start | bytes 589828
  11.9 4.7 %copy-start.1 = (f32[136,384]{1,0:T(8,128)}, f32[136,384]{1,0:T(8,128)S(1)}, u32[]{:S(2)}) copy-start(f32[136,384]{1,0:T(8,128)S(1)} %get-tuple-element.35.in_hbm) | copy-start | bytes 626692
  11.9 4.7 %copy-start.2 = (bf16[128,768]{1,0:T(8,128)(2,1)}, bf16[128,768]{1,0:T(8,128)(2,1)S(1)}, u32[]{:S(2)}) copy-start(bf16[128,768]{1,0:T(8,128)(2,1)S(1)} %get-tuple-element.36.scale_hbm) | copy-start | bytes 589828
  11.9 4.7 %copy-start.5 = (s32[12]{0:T(128)}, s32[12]{0:T(128)S(1)}, u32[]{:S(2)}) copy-start(s32[12]{0:T(128)S(1)} %get-tuple-element.26.slot_ref) | copy-start | bytes 148
  12.6 1.4 %collective-permute-start.4 = (bf16[32,3072]{1,0:T(8,128)(2,1)S(1)}, bf16[32,3072]{1,0:T(8,128)(2,1)S(1)}, u32[]{:S(2)}, u32[]{:S(2)}) collective-permute-start(bf16[32,3072]{1,0:T(8,128)(2,1)S(1)} %collective-permute-done.rest_1_), channel_id=1, source_target_pairs={{0,1},{1,0},{2,3},{3,2},{4,5},{5,4},{6,7},{7,6},{8,9},{9,8},{10,11... | collective-permute-start | bytes 589832 | tf_op jit(solution)/shard_map/ppermute | solution.py:305
  12.6 1.7 %collective-permute-start.5 = (bf16[32,3072]{1,0:T(8,128)(2,1)S(1)}, bf16[32,3072]{1,0:T(8,128)(2,1)S(1)}, u32[]{:S(2)}, u32[]{:S(2)}) collective-permute-start(bf16[32,3072]{1,0:T(8,128)(2,1)S(1)} %collective-permute-done.1.rest_2_), channel_id=1, source_target_pairs={{0,1},{1,0},{2,3},{3,2},{4,5},{5,4},{6,7},{7,6},{8,9},{9,8},{10,11... | collective-permute-start | bytes 589832 | tf_op jit(solution)/shard_map/ppermute | solution.py:305
  13.1 1.5 %collective-permute-start.6 = (bf16[32,3072]{1,0:T(8,128)(2,1)S(1)}, bf16[32,3072]{1,0:T(8,128)(2,1)S(1)}, u32[]{:S(2)}, u32[]{:S(2)}) collective-permute-start(bf16[32,3072]{1,0:T(8,128)(2,1)S(1)} %collective-permute-done.2.rest_3_), channel_id=1, source_target_pairs={{0,1},{1,0},{2,3},{3,2},{4,5},{5,4},{6,7},{7,6},{8,9},{9,8},{10,11... | collective-permute-start | bytes 589832 | tf_op jit(solution)/shard_map/ppermute | solution.py:305
  16.6 1.1 %copy-start = (bf16[256,3072]{1,0:T(8,128)(2,1)}, bf16[256,3072]{1,0:T(8,128)(2,1)S(1)}, u32[]{:S(2)}) copy-start(bf16[256,3072]{1,0:T(8,128)(2,1)S(1)} %get-tuple-element.34.proj_hbm) | copy-start | bytes 4718596
  17.8 25.1 %all-to-all-start = ((bf16[32,40,128]{2,1,0:T(8,128)(2,1)}), bf16[32,40,128]{2,1,0:T(8,128)(2,1)S(1)}, u32[]{:S(2)}, u32[]{:S(2)}) async-start(bf16[32,40,128]{2,1,0:T(8,128)(2,1)} %get-tuple-element.37), calls=%async_computation | async-start | bytes 655360 | tf_op jit(solution)/shard_map/all_to_all | solution.py:357
  43.7 17.8 %all-to-all-start.1 = ((bf16[32,32,128]{2,1,0:T(8,128)(2,1)}), bf16[32,32,128]{2,1,0:T(8,128)(2,1)S(1)}, u32[]{:S(2)}, u32[]{:S(2)}) async-start(bf16[32,32,128]{2,1,0:T(8,128)(2,1)} %prefix.1), calls=%async_computation.1 | async-start | bytes 524288 | tf_op jit(solution)/shard_map/all_to_all | solution.py:401
